TPU v7x, 32 devices: a whole 2x2x4 slice. The times are simulated.
32 devices in a mesh: rep: 8 (over y, x, core), shard: 4 (over z).
Axes of the slice: x: 2, y: 2, z: 4, core: 2. Of those that a mesh axis runs over, the one named last changes fastest.
Arguments:
- tokens: bfloat16 [16384, 1536], P(('rep', 'shard')), may hold values from -6 to 6
- cotangent: bfloat16 [16384, 1536], P(('rep', 'shard')), may hold values from -6 to 6
- norm_first: bfloat16 [1536], P('shard'), may hold values from 0.5 to 1.5
- branch_weight: bfloat16 [1536, 2048], P(None, 'shard'), may hold values from -0.15625 to 0.15625
- gelu_weight: bfloat16 [1536, 2048], P(None, 'shard'), may hold values from -0.15625 to 0.15625
- conv_weight: bfloat16 [4, 2048], P(None, 'shard'), may hold values from -2.5 to 2.5
- conv_bias: bfloat16 [2048], P('shard'), may hold values from -2.5 to 2.5
- gate_weight: bfloat16 [16, 128, 256], P('shard'), may hold values from -0.5 to 0.5
- gate_bias: bfloat16 [16, 256], P('shard'), may hold values from -2.5 to 2.5
- decay_param: bfloat16 [2048], P('shard'), may hold values from 2.1875 to 6.875
- merge_weight: bfloat16 [2048, 1536], P('shard'), may hold values from -0.375 to 0.375
- norm_second: bfloat16 [1536], P('shard'), may hold values from 0.5 to 1.5
- feed_gate: bfloat16 [1536, 4608], P(None, 'shard'), may hold values from -0.15625 to 0.15625
- feed_up: bfloat16 [1536, 4608], P(None, 'shard'), may hold values from -0.15625 to 0.15625
- feed_down: bfloat16 [4608, 1536], P('shard'), may hold values from -0.1875 to 0.1875
- down_branch: bfloat16 [1536, 128], P(None, 'shard'), may hold values from -0.15625 to 0.15625
- up_branch: bfloat16 [128, 2048], P('shard'), may hold values from -0.75 to 0.75
- down_gelu: bfloat16 [1536, 128], P(None, 'shard'), may hold values from -0.15625 to 0.15625
- up_gelu: bfloat16 [128, 2048], P('shard'), may hold values from -0.75 to 0.75
- down_gates: bfloat16 [2048, 128], P(None, 'shard'), may hold values from -0.125 to 0.125
- up_gates: bfloat16 [128, 4096], P('shard'), may hold values from -0.75 to 0.75
- down_merge: bfloat16 [2048, 128], P(None, 'shard'), may hold values from -0.125 to 0.125
- up_merge: bfloat16 [128, 1536], P('shard'), may hold values from -0.75 to 0.75
- down_feed_gate: bfloat16 [1536, 128], P(None, 'shard'), may hold values from -0.15625 to 0.15625
- up_feed_gate: bfloat16 [128, 4608], P('shard'), may hold values from -0.75 to 0.75
- down_feed_up: bfloat16 [1536, 128], P(None, 'shard'), may hold values from -0.15625 to 0.15625
- up_feed_up: bfloat16 [128, 4608], P('shard'), may hold values from -0.75 to 0.75
- down_feed_down: bfloat16 [4608, 128], P(None, 'shard'), may hold values from -0.09375 to 0.09375
- up_feed_down: bfloat16 [128, 1536], P('shard'), may hold values from -0.75 to 0.75
- seq_lengths: int32 [32, 4], P(('rep', 'shard')), may hold values from 1 to 256, 384 in all within a row
- adapter_index: int32 [32, 4], P(('rep', 'shard')), may hold values from 0 to 7
- deal_order: int32 [8, 2048], P('rep'), may hold values from 0 to 2047, as said below
Outputs:
- layer_out: float32 [16384, 1536], P(('rep', 'shard'))
- grad_tokens: float32 [16384, 1536], P(('rep', 'shard'))
- grad_down_branch: float32 [1536, 128], P(None, 'shard')
- grad_up_branch: float32 [128, 2048], P('shard')
- grad_down_gelu: float32 [1536, 128], P(None, 'shard')
- grad_up_gelu: float32 [128, 2048], P('shard')
- grad_down_gates: float32 [2048, 128], P(None, 'shard')
- grad_up_gates: float32 [128, 4096], P('shard')
- grad_down_merge: float32 [2048, 128], P(None, 'shard')
- grad_up_merge: float32 [128, 1536], P('shard')
- grad_down_feed_gate: float32 [1536, 128], P(None, 'shard')
- grad_up_feed_gate: float32 [128, 4608], P('shard')
- grad_down_feed_up: float32 [1536, 128], P(None, 'shard')
- grad_up_feed_up: float32 [128, 4608], P('shard')
- grad_down_feed_down: float32 [4608, 128], P(None, 'shard')
- grad_up_feed_down: float32 [128, 1536], P('shard')
Inputs may be any that keep to these rules, and one draw needn't show every extreme that they name: Each row of deal_order is a permutation of 0 to 2047. Exactly 128 of the arrival rows of one device (rows b * 512 to b * 512 + 511 of its group) fill slots of each block of its group. `seq_lengths`: in every block the lengths sum to 384 and the longest is 256.
All inputs are finite; a program needn't handle non-finite values.
Results may differ from a plain program's by a relative error of at most 0.015.
Values may be sent and summed in bfloat16 or wider, within the bound.
A program may use at most 320 MiB of HBM per device.

v0:
```python
import jax
import jax.numpy as jnp
from jax import lax
from jax.sharding import PartitionSpec as P

H = 16
DH = 128
NA = 8
R = 16


NORM_EPSILON = 1e-06
DECAY_SCALE = 8.0


def matmul(left, right):
    return jnp.dot(left, right, preferred_element_type=jnp.float32)


def matmul_right_t(left, right):
    return lax.dot_general(
        left, right, (((1,), (1,)), ((), ())), preferred_element_type=jnp.float32
    )


def matmul_left_t(left, right):
    return lax.dot_general(
        left, right, (((0,), (0,)), ((), ())), preferred_element_type=jnp.float32
    )


def root_norm(values, gain):
    return (
        values * lax.rsqrt(jnp.mean(values * values, axis=-1, keepdims=True) + NORM_EPSILON) * gain
    )


def layout(lengths_row, index_row, slots_count):
    seq_count = lengths_row.shape[0]
    ends = jnp.cumsum(lengths_row)
    starts = ends - lengths_row
    slots = jnp.arange(slots_count, dtype=jnp.int32)
    segment = jnp.sum((slots[:, None] >= ends[None, :]).astype(jnp.int32), axis=1)
    start_all = jnp.concatenate([starts, ends[-1:]])
    member = segment[:, None] == jnp.arange(seq_count + 1, dtype=jnp.int32)[None, :]
    position = slots - jnp.sum(jnp.where(member, start_all[None, :], 0), axis=1)
    live_rows = segment < seq_count
    chosen = jnp.sum(jnp.where(member[:, :seq_count], index_row[None, :], 0), axis=1)
    adapter_hit = (chosen[:, None] == jnp.arange(NA, dtype=jnp.int32)[None, :]) & live_rows[:, None]
    adapter_mask = jnp.repeat(adapter_hit.astype(jnp.float32), R, axis=1)
    return (position, live_rows.astype(jnp.float32), adapter_mask)


def conv_apply(values, weight, bias, position):
    total = bias[None, :] + weight[0][None, :] * values
    for offset in range(1, weight.shape[0]):
        moved = jnp.concatenate(
            [jnp.zeros((offset, values.shape[1]), values.dtype), values[:-offset]], axis=0
        )
        keeper = (position >= offset).astype(values.dtype)[:, None]
        total = total + weight[offset][None, :] * moved * keeper
    return total


def combine(earlier, later):
    return (earlier[0] * later[0], later[0] * earlier[1] + later[1])


def recurrence(gate_logits, conv_out, gelu_in, decay, position):
    rows_count = conv_out.shape[0]
    shaped = gate_logits.reshape(rows_count, H, 2 * DH)
    input_gate = jax.nn.sigmoid(shaped[:, :, :DH]).reshape(rows_count, H * DH)
    rec_gate = jax.nn.sigmoid(shaped[:, :, DH:]).reshape(rows_count, H * DH)
    log_decay = -DECAY_SCALE * rec_gate * jax.nn.softplus(-decay)[None, :]
    decay_now = jnp.exp(log_decay)
    first = (position == 0)[:, None]
    scale_in = jnp.where(first, 1.0, jnp.sqrt(-jnp.expm1(2.0 * log_decay)))
    carried = jnp.where(first, 0.0, decay_now)
    driven = scale_in * input_gate * conv_out
    unused, state = lax.associative_scan(combine, (carried, driven), axis=0)
    return state * jax.nn.gelu(gelu_in)


def feed_mix(hidden_gate, hidden_up):
    return jax.nn.gelu(hidden_gate) * hidden_up


def local(
    tokens,
    cotangent,
    norm_first,
    branch_weight,
    gelu_weight,
    conv_weight,
    conv_bias,
    gate_weight,
    gate_bias,
    decay_param,
    merge_weight,
    norm_second,
    feed_gate,
    feed_up,
    feed_down,
    down_branch,
    up_branch,
    down_gelu,
    up_gelu,
    down_gates,
    up_gates,
    down_merge,
    up_merge,
    down_feed_gate,
    up_feed_gate,
    down_feed_up,
    up_feed_up,
    down_feed_down,
    up_feed_down,
    seq_lengths,
    adapter_index,
    deal_order,
):
    rows_here = tokens.shape[0]
    shards = lax.axis_size("shard")
    my_index = lax.axis_index("shard")
    deal_row = deal_order[0]
    group_rows = deal_row.shape[0]
    gathered = (
        lax.all_gather(tokens, "shard", axis=0, tiled=True),
        lax.all_gather(cotangent, "shard", axis=0, tiled=True),
    )
    my_picks = lax.dynamic_slice_in_dim(deal_row, my_index * rows_here, rows_here)
    work_in = jnp.take(gathered[0], my_picks, axis=0)
    work_cot = jnp.take(gathered[1], my_picks, axis=0)
    block_parts = (
        lax.all_gather(norm_first, "shard", axis=0, tiled=True),
        lax.all_gather(branch_weight, "shard", axis=1, tiled=True),
        lax.all_gather(gelu_weight, "shard", axis=1, tiled=True),
        lax.all_gather(conv_weight, "shard", axis=1, tiled=True),
        lax.all_gather(conv_bias, "shard", axis=0, tiled=True),
        lax.all_gather(gate_weight, "shard", axis=0, tiled=True),
        lax.all_gather(gate_bias, "shard", axis=0, tiled=True),
        lax.all_gather(decay_param, "shard", axis=0, tiled=True),
        lax.all_gather(merge_weight, "shard", axis=0, tiled=True),
    )
    (
        gain_first,
        weight_branch,
        weight_gelu,
        taps_conv,
        bias_conv,
        weight_gates,
        bias_gates,
        decay_all,
        weight_merge,
    ) = block_parts
    adapter_parts = (
        lax.all_gather(down_branch, "shard", axis=1, tiled=True),
        lax.all_gather(up_branch, "shard", axis=0, tiled=True),
        lax.all_gather(down_gelu, "shard", axis=1, tiled=True),
        lax.all_gather(up_gelu, "shard", axis=0, tiled=True),
        lax.all_gather(down_gates, "shard", axis=1, tiled=True),
        lax.all_gather(up_gates, "shard", axis=0, tiled=True),
        lax.all_gather(down_merge, "shard", axis=1, tiled=True),
        lax.all_gather(up_merge, "shard", axis=0, tiled=True),
        lax.all_gather(down_feed_gate, "shard", axis=1, tiled=True),
        lax.all_gather(up_feed_gate, "shard", axis=0, tiled=True),
        lax.all_gather(down_feed_up, "shard", axis=1, tiled=True),
        lax.all_gather(up_feed_up, "shard", axis=0, tiled=True),
        lax.all_gather(down_feed_down, "shard", axis=1, tiled=True),
        lax.all_gather(up_feed_down, "shard", axis=0, tiled=True),
    )
    (
        fact_down_branch,
        fact_up_branch,
        fact_down_gelu,
        fact_up_gelu,
        fact_down_gates,
        fact_up_gates,
        fact_down_merge,
        fact_up_merge,
        fact_down_fgate,
        fact_up_fgate,
        fact_down_fup,
        fact_up_fup,
        fact_down_fdown,
        fact_up_fdown,
    ) = adapter_parts
    position, live_rows, adapter_mask = layout(seq_lengths[0], adapter_index[0], rows_here)

    def adapter_forward(act, down, up):
        rank_part = (matmul(act, down) * adapter_mask).astype(jnp.bfloat16)
        return (rank_part, matmul(rank_part, up))

    def adapter_backward(grad_low, act, rank_part, up):
        grad_rank = (matmul_right_t(grad_low, up) * adapter_mask).astype(jnp.bfloat16)
        return (grad_rank, matmul_left_t(act, grad_rank), matmul_left_t(rank_part, grad_low))

    gain_first_f = gain_first.astype(jnp.float32)
    rows_in = work_in.astype(jnp.float32)
    normed_first, first_pull = jax.vjp(lambda values: root_norm(values, gain_first_f), rows_in)
    act_first = normed_first.astype(jnp.bfloat16)
    rank_branch, extra_branch = adapter_forward(act_first, fact_down_branch, fact_up_branch)
    branch = matmul(act_first, weight_branch) + extra_branch
    rank_gelu, extra_gelu = adapter_forward(act_first, fact_down_gelu, fact_up_gelu)
    gelu_in = matmul(act_first, weight_gelu) + extra_gelu
    taps_f = taps_conv.astype(jnp.float32)
    bias_f = bias_conv.astype(jnp.float32)
    conv_out, conv_pull = jax.vjp(
        lambda values: conv_apply(values, taps_f, bias_f, position), branch
    )
    conv_low = conv_out.astype(jnp.bfloat16)
    heads = conv_low.reshape(rows_here, H, DH)
    blockwise = jnp.einsum(
        "thd,hde->the", heads, weight_gates, preferred_element_type=jnp.float32
    ).reshape(rows_here, 2 * H * DH)
    rank_gates, extra_gates = adapter_forward(conv_low, fact_down_gates, fact_up_gates)
    gate_logits = blockwise + bias_gates.astype(jnp.float32).reshape(-1)[None, :] + extra_gates
    decay_f = decay_all.astype(jnp.float32)
    mixed, mixed_pull = jax.vjp(
        lambda logits, conv_in, gelu_part: recurrence(
            logits, conv_in, gelu_part, decay_f, position
        ),
        gate_logits,
        conv_out,
        gelu_in,
    )
    mixed_low = mixed.astype(jnp.bfloat16)
    rank_merge, extra_merge = adapter_forward(mixed_low, fact_down_merge, fact_up_merge)
    resid = rows_in + matmul(mixed_low, weight_merge) + extra_merge
    feed_parts = (
        lax.all_gather(norm_second, "shard", axis=0, tiled=True),
        lax.all_gather(feed_gate, "shard", axis=1, tiled=True),
        lax.all_gather(feed_up, "shard", axis=1, tiled=True),
        lax.all_gather(feed_down, "shard", axis=0, tiled=True),
    )
    gain_second, weight_fgate, weight_fup, weight_fdown = feed_parts
    gain_second_f = gain_second.astype(jnp.float32)
    normed_second, second_pull = jax.vjp(lambda values: root_norm(values, gain_second_f), resid)
    act_second = normed_second.astype(jnp.bfloat16)
    rank_fgate, extra_fgate = adapter_forward(act_second, fact_down_fgate, fact_up_fgate)
    hidden_gate = matmul(act_second, weight_fgate) + extra_fgate
    rank_fup, extra_fup = adapter_forward(act_second, fact_down_fup, fact_up_fup)
    hidden_up = matmul(act_second, weight_fup) + extra_fup
    hidden, hidden_pull = jax.vjp(feed_mix, hidden_gate, hidden_up)
    hidden_low = hidden.astype(jnp.bfloat16)
    rank_fdown, extra_fdown = adapter_forward(hidden_low, fact_down_fdown, fact_up_fdown)
    work_out = (resid + matmul(hidden_low, weight_fdown) + extra_fdown) * live_rows[:, None]
    grad_out = work_cot.astype(jnp.float32) * live_rows[:, None]
    grad_out_low = grad_out.astype(jnp.bfloat16)
    grad_rank_fdown, grad_down_fdown, grad_up_fdown = adapter_backward(
        grad_out_low, hidden_low, rank_fdown, fact_up_fdown
    )
    grad_hidden = matmul_right_t(grad_out_low, weight_fdown) + matmul_right_t(
        grad_rank_fdown, fact_down_fdown
    )
    grad_hgate, grad_hup = hidden_pull(grad_hidden)
    grad_hgate_low = grad_hgate.astype(jnp.bfloat16)
    grad_hup_low = grad_hup.astype(jnp.bfloat16)
    grad_rank_fgate, grad_down_fgate, grad_up_fgate = adapter_backward(
        grad_hgate_low, act_second, rank_fgate, fact_up_fgate
    )
    grad_rank_fup, grad_down_fup, grad_up_fup = adapter_backward(
        grad_hup_low, act_second, rank_fup, fact_up_fup
    )
    grad_second = (
        matmul_right_t(grad_hgate_low, weight_fgate)
        + matmul_right_t(grad_hup_low, weight_fup)
        + matmul_right_t(grad_rank_fgate, fact_down_fgate)
        + matmul_right_t(grad_rank_fup, fact_down_fup)
    )
    grad_resid = grad_out + second_pull(grad_second)[0]
    grad_resid_low = grad_resid.astype(jnp.bfloat16)
    grad_rank_merge, grad_down_merge, grad_up_merge = adapter_backward(
        grad_resid_low, mixed_low, rank_merge, fact_up_merge
    )
    grad_mixed = matmul_right_t(grad_resid_low, weight_merge) + matmul_right_t(
        grad_rank_merge, fact_down_merge
    )
    grad_logits, grad_conv_direct, grad_gelu_in = mixed_pull(grad_mixed)
    grad_logits_low = grad_logits.astype(jnp.bfloat16)
    grad_rank_gates, grad_down_gates, grad_up_gates = adapter_backward(
        grad_logits_low, conv_low, rank_gates, fact_up_gates
    )
    grad_heads = jnp.einsum(
        "the,hde->thd",
        grad_logits_low.reshape(rows_here, H, 2 * DH),
        weight_gates,
        preferred_element_type=jnp.float32,
    ).reshape(rows_here, H * DH)
    grad_conv = grad_conv_direct + grad_heads + matmul_right_t(grad_rank_gates, fact_down_gates)
    grad_branch = conv_pull(grad_conv)[0]
    grad_branch_low = grad_branch.astype(jnp.bfloat16)
    grad_gelu_low = grad_gelu_in.astype(jnp.bfloat16)
    grad_rank_branch, grad_down_branch, grad_up_branch = adapter_backward(
        grad_branch_low, act_first, rank_branch, fact_up_branch
    )
    grad_rank_gelu, grad_down_gelu, grad_up_gelu = adapter_backward(
        grad_gelu_low, act_first, rank_gelu, fact_up_gelu
    )
    grad_first = (
        matmul_right_t(grad_branch_low, weight_branch)
        + matmul_right_t(grad_gelu_low, weight_gelu)
        + matmul_right_t(grad_rank_branch, fact_down_branch)
        + matmul_right_t(grad_rank_gelu, fact_down_gelu)
    )
    grad_work = grad_resid + first_pull(grad_first)[0]
    collected = (
        lax.all_gather(work_out, "shard", axis=0, tiled=True),
        lax.all_gather(grad_work, "shard", axis=0, tiled=True),
    )
    inverse = (
        jnp.zeros((group_rows,), jnp.int32)
        .at[deal_row]
        .set(jnp.arange(group_rows, dtype=jnp.int32))
    )
    my_rows = lax.dynamic_slice_in_dim(inverse, my_index * rows_here, rows_here)
    layer_out = jnp.take(collected[0], my_rows, axis=0)
    grad_tokens = jnp.take(collected[1], my_rows, axis=0)
    part_width = grad_down_branch.shape[1] // shards
    summed = lax.psum(
        (
            grad_down_branch,
            grad_up_branch,
            grad_down_gelu,
            grad_up_gelu,
            grad_down_gates,
            grad_up_gates,
            grad_down_merge,
            grad_up_merge,
            grad_down_fgate,
            grad_up_fgate,
            grad_down_fup,
            grad_up_fup,
            grad_down_fdown,
            grad_up_fdown,
        ),
        ("rep", "shard"),
    )
    owned = tuple(
        (
            lax.dynamic_slice_in_dim(
                summed[number], my_index * part_width, part_width, 1 - number % 2
            )
            for number in range(14)
        )
    )
    return (
        layer_out,
        grad_tokens,
        owned[0],
        owned[1],
        owned[2],
        owned[3],
        owned[4],
        owned[5],
        owned[6],
        owned[7],
        owned[8],
        owned[9],
        owned[10],
        owned[11],
        owned[12],
        owned[13],
    )


def solution(mesh):
    in_specs = (
        P(("rep", "shard"), None),
        P(("rep", "shard"), None),
        P("shard"),
        P(None, "shard"),
        P(None, "shard"),
        P(None, "shard"),
        P("shard"),
        P("shard", None, None),
        P("shard", None),
        P("shard"),
        P("shard", None),
        P("shard"),
        P(None, "shard"),
        P(None, "shard"),
        P("shard", None),
        P(None, "shard"),
        P("shard", None),
        P(None, "shard"),
        P("shard", None),
        P(None, "shard"),
        P("shard", None),
        P(None, "shard"),
        P("shard", None),
        P(None, "shard"),
        P("shard", None),
        P(None, "shard"),
        P("shard", None),
        P(None, "shard"),
        P("shard", None),
        P(("rep", "shard"), None),
        P(("rep", "shard"), None),
        P("rep", None),
    )
    out_specs = (
        P(("rep", "shard"), None),
        P(("rep", "shard"), None),
        P(None, "shard"),
        P("shard", None),
        P(None, "shard"),
        P("shard", None),
        P(None, "shard"),
        P("shard", None),
        P(None, "shard"),
        P("shard", None),
        P(None, "shard"),
        P("shard", None),
        P(None, "shard"),
        P("shard", None),
        P(None, "shard"),
        P("shard", None),
    )
    return jax.shard_map(local, mesh=mesh, in_specs=in_specs, out_specs=out_specs, check_vma=False)
```

profile of v0, /device:TPU:0, one launch (start us, length us, event | category | flops | bytes accessed | tf_op | source)
XLA Modules:
  0.0 3010.7 jit_solution(17063541124897532782)
XLA Ops:
  19.0 15.6 all-gather.1
  35.0 17.7 all_gather.98
  52.7 23.4 all_gather.99
  76.9 16.7 all_gather.95
  93.6 14.6 all-gather
  108.3 20.1 all_gather.102
  128.4 15.4 all-gather.2
  143.8 12.0 all-gather.3
  156.5 17.4 all_gather.106
  173.8 23.5 all_gather.107
  197.3 24.9 all_gather.109
  222.2 22.7 all_gather.110
  244.9 12.1 all-gather.4
  257.6 20.8 all_gather.116
  278.3 22.4 all_gather.113
  300.7 15.7 all_gather.120
  398.6 11.7 exponential_select_fusion
  410.3 9.8 slice.325
  556.8 10.1 slice.323
  567.0 10.1 slice.388
  616.8 16.5 pad.367
  639.2 16.5 pad.366
  678.8 31.1 %all-gather.47.cloned.1.call-done = bf16[2048,1536]{1,0:T(8,128)(2,1)} async-done(((bf16[512,1536]{1,0:T(8,128)(2,1)}), bf16[2048,1536]{1,0:T(8,128)(2,1)}) %all-gather.47.cloned.1.call-update) | async-done | bytes 6291472 | tf_op jit(solution)/shard_map/all_gather | solution.py:129
  720.8 232.9 %all-gather.37.cloned.1.call-done = bf16[1536,4608]{1,0:T(8,128)(2,1)} async-done(((bf16[1536,1152]{1,0:T(8,128)(2,1)}), bf16[1536,4608]{1,0:T(8,128)(2,1)}) %all-gather.37.cloned.1.call-update) | async-done | bytes 14155792 | tf_op jit(solution)/shard_map/all_gather | solution.py:233
  953.6 12.8 fusion.130
  966.5 230.9 %all-gather.33.cloned.1.call-done = bf16[1536,4608]{1,0:T(8,128)(2,1)} async-done(((bf16[1536,1152]{1,0:T(8,128)(2,1)}), bf16[1536,4608]{1,0:T(8,128)(2,1)}) %all-gather.33.cloned.1.call-update) | async-done | bytes 14155792 | tf_op jit(solution)/shard_map/all_gather | solution.py:232
  1197.4 12.8 fusion.129
  1210.2 17.2 all-gather.39.cloned.1.call-done
  1236.4 22.2 all-gather.35.cloned.1.call-done
  1258.6 10.0 convolution_add_fusion.2
  1268.6 234.5 %all-gather.41.cloned.1.call-done = bf16[4608,1536]{1,0:T(8,128)(2,1)} async-done(((bf16[1152,1536]{1,0:T(8,128)(2,1)}), bf16[4608,1536]{1,0:T(8,128)(2,1)}) %all-gather.41.cloned.1.call-update) | async-done | bytes 14155792 | tf_op jit(solution)/shard_map/all_gather | solution.py:234
  1503.1 13.4 fusion.95
  1516.5 16.8 all-gather.43.cloned.1.call-done
  1533.3 17.2 multiply_convert_fusion
  1550.6 13.4 fusion.131
  1565.4 10.3 convolution_add_fusion.12
  1750.2 11.2 multiply_add_fusion.1
  1764.3 16.6 pad.426
  1781.0 16.5 pad.427
  1797.5 16.6 pad.451
  1814.0 16.6 pad.452
  1830.6 16.9 pad.370
  1847.6 16.9 pad.428
  1864.5 18.5 multiply_multiply_fusion.5
  1977.7 12.4 convolution_add_fusion.13
  2020.2 528.2 %all-reduce.96.cloned.1.call-done = (f32[1536,128]{0,1:T(8,128)}, f32[128,2048]{1,0:T(8,128)}, f32[1536,128]{0,1:T(8,128)}, f32[128,2048]{1,0:T(8,128)}, f32[204...) async-done(((f32[1536,128]{0,1:T(8,128)}, ...) | async-done | bytes 18087952 | tf_op jit(solution)/shard_map/psum | solution.py:320
  2563.9 207.1 %all-gather.45.cloned.1.call-done = f32[2048,1536]{1,0:T(8,128)} async-done(((f32[512,1536]{1,0:T(8,128)}), f32[2048,1536]{1,0:T(8,128)}) %all-gather.45.cloned.1.call-update) | async-done | bytes 12582928 | tf_op jit(solution)/shard_map/all_gather | solution.py:308
  2779.2 210.2 %all-gather.49.cloned.1.call-done = f32[2048,1536]{1,0:T(8,128)} async-done(((f32[512,1536]{1,0:T(8,128)}), f32[2048,1536]{1,0:T(8,128)}) %all-gather.49.cloned.1.call-update) | async-done | bytes 12582928 | tf_op jit(solution)/shard_map/all_gather | solution.py:309
  (813 shorter events, 660.5 us)
Async XLA Ops:
  7.2 311.1 %all-gather.21.cloned.1.call-start = ((), (), s32[]{:S(2)}) async-start(), calls=%async_computation | async-start | bytes 7864320 | tf_op jit(solution)/shard_map/all_gather | solution.py:128
  7.9 321.5 %all-gather.23.cloned.1.call-start = ((), (), s32[]{:S(2)}) async-start(), calls=%async_computation.1 | async-start | bytes 7864320 | tf_op jit(solution)/shard_map/all_gather | solution.py:136
  8.7 332.8 %all-gather.25.cloned.1.call-start = ((), (), s32[]{:S(2)}) async-start(), calls=%async_computation.2 | async-start | bytes 1310720 | tf_op jit(solution)/shard_map/all_gather | solution.py:140
  9.4 354.0 %all-gather.27.cloned.1.call-start = ((), (), s32[]{:S(2)}) async-start(), calls=%async_computation.3 | async-start | bytes 1310720 | tf_op jit(solution)/shard_map/all_gather | solution.py:162
  10.0 646.4 %all-gather.29.cloned.1.call-start = ((), (), s32[]{:S(2)}) async-start(), calls=%async_computation.4 | async-start | bytes 7864320 | tf_op jit(solution)/shard_map/all_gather | solution.py:137
  10.6 658.0 %all-gather.31.cloned.1.call-start = ((), (), s32[]{:S(2)}) async-start(), calls=%async_computation.5 | async-start | bytes 7864320 | tf_op jit(solution)/shard_map/all_gather | solution.py:143
  11.1 698.7 %all-gather.47.cloned.1.call-start = ((), (), s32[]{:S(2)}) async-start(), calls=%async_computation.13 | async-start | bytes 7864320 | tf_op jit(solution)/shard_map/all_gather | solution.py:129
  11.9 941.7 %all-gather.37.cloned.1.call-start = ((), (), s32[]{:S(2)}) async-start(), calls=%async_computation.8 | async-start | bytes 17694720 | tf_op jit(solution)/shard_map/all_gather | solution.py:233
  12.7 64.2 %copy-start.204 = (bf16[4,512]{1,0:T(4,128)(2,1)S(1)}, bf16[4,512]{1,0:T(4,128)(2,1)}, u32[]{:S(2)}) copy-start(bf16[4,512]{1,0:T(4,128)(2,1)} %param.41) | copy-start | bytes 12292
  12.7 80.9 %copy-start.206 = (bf16[512]{0:T(512)(128)(2,1)S(1)}, bf16[512]{0:T(512)(128)(2,1)}, u32[]{:S(2)}) copy-start(bf16[512]{0:T(512)(128)(2,1)} %param.42) | copy-start | bytes 3076
  12.7 1184.6 %all-gather.33.cloned.1.call-start = ((), (), s32[]{:S(2)}) async-start(), calls=%async_computation.6 | async-start | bytes 17694720 | tf_op jit(solution)/shard_map/all_gather | solution.py:232
  13.4 94.8 %copy-start.158 = (bf16[2048,32]{0,1:T(8,128)(2,1)S(1)}, bf16[2048,32]{0,1:T(8,128)(2,1)}, u32[]{:S(2)}) copy-start(bf16[2048,32]{0,1:T(8,128)(2,1)} %param.55) | copy-start | bytes 393220
  13.5 114.9 %copy-start.205 = (bf16[4,256]{1,0:T(4,128)(2,1)S(1)}, bf16[4,256]{1,0:T(4,128)(2,1)}, u32[]{:S(2)}) copy-start(bf16[4,256]{1,0:T(4,128)(2,1)} %param.44) | copy-start | bytes 6148
  13.5 130.4 %copy-start.207 = (bf16[512]{0:T(512)(128)(2,1)S(1)}, bf16[512]{0:T(512)(128)(2,1)}, u32[]{:S(2)}) copy-start(bf16[512]{0:T(512)(128)(2,1)} %param.45) | copy-start | bytes 3076
  13.5 143.0 %copy-start.169 = (bf16[1536,32]{0,1:T(8,128)(2,1)S(1)}, bf16[1536,32]{0,1:T(8,128)(2,1)}, u32[]{:S(2)}) copy-start(bf16[1536,32]{0,1:T(8,128)(2,1)} %param.53) | copy-start | bytes 294916
  13.5 160.3 %copy-start.159 = (bf16[32,2048]{1,0:T(8,128)(2,1)S(1)}, bf16[32,2048]{1,0:T(8,128)(2,1)}, u32[]{:S(2)}) copy-start(bf16[32,2048]{1,0:T(8,128)(2,1)} %param.54) | copy-start | bytes 393220
  13.5 1213.9 %all-gather.39.cloned.1.call-start = ((), (), s32[]{:S(2)}) async-start(), calls=%async_computation.9 | async-start | bytes 1474560 | tf_op jit(solution)/shard_map/all_gather | solution.py:168
  14.1 183.2 %copy-start.160 = (bf16[2048,32]{0,1:T(8,128)(2,1)S(1)}, bf16[2048,32]{0,1:T(8,128)(2,1)}, u32[]{:S(2)}) copy-start(bf16[2048,32]{0,1:T(8,128)(2,1)} %param.57) | copy-start | bytes 393220
  14.1 1244.5 %all-gather.35.cloned.1.call-start = ((), (), s32[]{:S(2)}) async-start(), calls=%async_computation.7 | async-start | bytes 1474560 | tf_op jit(solution)/shard_map/all_gather | solution.py:166
  14.8 207.3 %copy-start.170 = (bf16[32,1536]{1,0:T(8,128)(2,1)S(1)}, bf16[32,1536]{1,0:T(8,128)(2,1)}, u32[]{:S(2)}) copy-start(bf16[32,1536]{1,0:T(8,128)(2,1)} %param.58) | copy-start | bytes 294916
  14.8 230.0 %copy-start.209 = (bf16[384]{0:T(512)(128)(2,1)S(1)}, bf16[384]{0:T(512)(128)(2,1)}, u32[]{:S(2)}) copy-start(bf16[384]{0:T(512)(128)(2,1)} %param.47) | copy-start | bytes 2308
  14.9 242.7 %copy-start.171 = (bf16[1536,32]{0,1:T(8,128)(2,1)S(1)}, bf16[1536,32]{0,1:T(8,128)(2,1)}, u32[]{:S(2)}) copy-start(bf16[1536,32]{0,1:T(8,128)(2,1)} %param.61) | copy-start | bytes 294916
  14.9 263.5 %copy-start.172 = (bf16[1536,32]{0,1:T(8,128)(2,1)S(1)}, bf16[1536,32]{0,1:T(8,128)(2,1)}, u32[]{:S(2)}) copy-start(bf16[1536,32]{0,1:T(8,128)(2,1)} %param.59) | copy-start | bytes 294916
  14.9 285.8 %copy-start.173 = (bf16[32,1536]{1,0:T(8,128)(2,1)S(1)}, bf16[32,1536]{1,0:T(8,128)(2,1)}, u32[]{:S(2)}) copy-start(bf16[32,1536]{1,0:T(8,128)(2,1)} %param.64) | copy-start | bytes 294916
  14.9 1488.2 %all-gather.41.cloned.1.call-start = ((), (), s32[]{:S(2)}) async-start(), calls=%async_computation.10 | async-start | bytes 17694720 | tf_op jit(solution)/shard_map/all_gather | solution.py:234
  15.5 1517.9 %all-gather.43.cloned.1.call-start = ((), (), s32[]{:S(2)}) async-start(), calls=%async_computation.11 | async-start | bytes 1474560 | tf_op jit(solution)/shard_map/all_gather | solution.py:169
  16.2 2532.2 %all-reduce.96.cloned.1.call-start = ((), (), s32[]{:S(2)}) async-start(), calls=%async_computation.15 | async-start | bytes 36175872 | tf_op jit(solution)/shard_map/psum | solution.py:320
  34.7 292.1 %copy-start.177 = (f32[1536]{0:T(1024)}, f32[1536]{0:T(1024)S(1)}, u32[]{:S(2)}) copy-start(f32[1536]{0:T(1024)S(1)} %reshape.246) | copy-start | bytes 18436
  52.7 276.1 %copy-start.72 = (bf16[1536,128]{0,1:T(8,128)(2,1)}, bf16[1536,128]{0,1:T(8,128)(2,1)S(1)}, u32[]{:S(2)}) copy-start(bf16[1536,128]{0,1:T(8,128)(2,1)S(1)} %all_gather.98) | copy-start | bytes 1179652
  76.0 258.9 %copy-start.49 = (bf16[128,2048]{1,0:T(8,128)(2,1)}, bf16[128,2048]{1,0:T(8,128)(2,1)S(1)}, u32[]{:S(2)}) copy-start(bf16[128,2048]{1,0:T(8,128)(2,1)S(1)} %all_gather.99) | copy-start | bytes 1572868
  76.8 321.8 %copy-start.198 = (pred[512]{0:T(512)(128)(4,1)}, pred[512]{0:T(512)(128)(4,1)S(1)}, u32[]{:S(2)}) copy-start(pred[512]{0:T(512)(128)(4,1)S(1)} %get-tuple-element.146) | copy-start | bytes 1540
  93.6 242.1 %copy-start.175 = (f32[1,2048]{1,0:T(1,128)}, f32[1,2048]{1,0:T(1,128)S(1)}, u32[]{:S(2)}) copy-start(f32[1,2048]{1,0:T(1,128)S(1)} %get-tuple-element.140) | copy-start | bytes 24580
  93.6 242.1 %copy-start.179 = (f32[1,2048]{1,0:T(1,128)}, f32[1,2048]{1,0:T(1,128)S(1)}, u32[]{:S(2)}) copy-start(f32[1,2048]{1,0:T(1,128)S(1)} %get-tuple-element.141) | copy-start | bytes 24580
  93.6 242.1 %copy-start.181 = (f32[1,2048]{1,0:T(1,128)}, f32[1,2048]{1,0:T(1,128)S(1)}, u32[]{:S(2)}) copy-start(f32[1,2048]{1,0:T(1,128)S(1)} %get-tuple-element.143) | copy-start | bytes 24580
  93.6 242.1 %copy-start.183 = (f32[1,2048]{1,0:T(1,128)}, f32[1,2048]{1,0:T(1,128)S(1)}, u32[]{:S(2)}) copy-start(f32[1,2048]{1,0:T(1,128)S(1)} %get-tuple-element.142) | copy-start | bytes 24580
  128.3 228.6 %copy-start.46 = (bf16[2048,128]{0,1:T(8,128)(2,1)}, bf16[2048,128]{0,1:T(8,128)(2,1)S(1)}, u32[]{:S(2)}) copy-start(bf16[2048,128]{0,1:T(8,128)(2,1)S(1)} %all_gather.102) | copy-start | bytes 1572868
  156.5 242.2 %copy-start.151 = (f32[2048]{0:T(1024)}, f32[2048]{0:T(1024)S(1)}, u32[]{:S(2)}) copy-start(f32[2048]{0:T(1024)S(1)} %get-tuple-element.145) | copy-start | bytes 24580
  328.8 327.6 %copy-start.12 = (bf16[512,1536]{1,0:T(8,128)(2,1)}, bf16[512,1536]{1,0:T(8,128)(2,1)S(1)}, u32[]{:S(2)}) copy-start(bf16[512,1536]{1,0:T(8,128)(2,1)S(1)} %fusion.33) | copy-start | bytes 4718596
  508.5 47.4 %copy-start.126 = (f32[8,2048]{1,0:T(8,128)}, f32[8,2048]{1,0:T(8,128)S(1)}, u32[]{:S(2)}) copy-start(f32[8,2048]{1,0:T(8,128)S(1)} %slice.354) | copy-start | bytes 196612
  528.7 50.0 %copy-start.128 = (f32[7,2048]{1,0:T(8,128)}, f32[7,2048]{1,0:T(8,128)S(1)}, u32[]{:S(2)}) copy-start(f32[7,2048]{1,0:T(8,128)S(1)} %slice.353) | copy-start | bytes 172036
  531.0 48.5 %copy-start.109 = (f32[15,2048]{1,0:T(8,128)}, f32[15,2048]{1,0:T(8,128)S(1)}, u32[]{:S(2)}) copy-start(f32[15,2048]{1,0:T(8,128)S(1)} %slice.347) | copy-start | bytes 368644
  677.6 519.7 %copy-start.14 = (bf16[512,1536]{1,0:T(8,128)(2,1)}, bf16[512,1536]{1,0:T(8,128)(2,1)S(1)}, u32[]{:S(2)}) copy-start(bf16[512,1536]{1,0:T(8,128)(2,1)S(1)} %multiply_convert_fusion.3) | copy-start | bytes 4718596
  678.2 549.2 %copy-start.92 = (bf16[512,128]{1,0:T(8,128)(2,1)}, bf16[512,128]{1,0:T(8,128)(2,1)S(1)}, u32[]{:S(2)}) copy-start(bf16[512,128]{1,0:T(8,128)(2,1)S(1)} %fusion.49) | copy-start | bytes 393220
  678.8 579.8 %copy-start.94 = (bf16[512,128]{1,0:T(8,128)(2,1)}, bf16[512,128]{1,0:T(8,128)(2,1)S(1)}, u32[]{:S(2)}) copy-start(bf16[512,128]{1,0:T(8,128)(2,1)S(1)} %fusion.48) | copy-start | bytes 393220
  720.8 812.6 %copy-start.155 = (bf16[512,128]{1,0:T(8,128)(2,1)}, bf16[512,128]{1,0:T(8,128)(2,1)S(1)}, u32[]{:S(2)}) copy-start(bf16[512,128]{1,0:T(8,128)(2,1)S(1)} %fusion.50) | copy-start | bytes 393220
  1236.4 266.7 %copy-start.42 = (bf16[512,1536]{1,0:T(8,128)(2,1)S(1)}, bf16[512,1536]{1,0:T(8,128)(2,1)}, u32[]{:S(2)}) copy-start(bf16[512,1536]{1,0:T(8,128)(2,1)} %gather_fusion.2) | copy-start | bytes 4718596
  1975.9 795.1 %all-gather.45.cloned.1.call-start = ((), (), s32[]{:S(2)}) async-start(), calls=%async_computation.12 | async-start | bytes 15728640 | tf_op jit(solution)/shard_map/all_gather | solution.py:308
  1993.2 996.2 %all-gather.49.cloned.1.call-start = ((), (), s32[]{:S(2)}) async-start(), calls=%async_computation.14 | async-start | bytes 15728640 | tf_op jit(solution)/shard_map/all_gather | solution.py:309
  (193 other events, 1690.1 us)
Sparse Core Ops, SparseCore 0:
  9.6 143.8 all-gather.20
  155.0 150.7 all-gather.22
  307.4 26.5 all-gather.24
  335.4 27.9 all-gather.26
  364.8 114.8 all-gather.28
  481.1 113.5 all-gather.30
  596.3 113.5 all-gather.46
  711.4 242.1 all-gather.36
  955.2 242.1 all-gather.32
  1198.8 28.6 all-gather.38
  1229.0 29.5 all-gather.34
  1260.0 243.0 all-gather.40
  1504.7 28.6 all-gather.42
  1976.0 572.3 all-reduce.95
  2551.4 219.4 all-gather.44
  2773.0 216.3 all-gather.48
where the time goes:
time: 3020 us; the launch traced here: 3010 us
  waiting for transfers between devices  1740 us (58%)
  local copies, waits for them, and re-layouts  544 us (18%)
  blocking collectives  295 us (10%)
  matrix products  234 us (8%)
  other arithmetic  177 us (6%)
    psum x1, waiting for transfers between devices, local(): lax.psum((grad_down_branch, grad_up_branch, grad_down_gelu, grad_up_gelu,...  528 us
    pad x70, local copies, waits for them, and re-layouts, recurrence(): unused, state = lax.associative_scan(combine, (carried, driven), axis=0)  244 us
    all_gather x1, waiting for transfers between devices, local(): lax.all_gather(feed_down, 'shard', axis=0, tiled=True)  234 us
    all_gather x1, waiting for transfers between devices, local(): lax.all_gather(feed_up, 'shard', axis=1, tiled=True)  233 us
    all_gather x1, waiting for transfers between devices, local(): lax.all_gather(feed_gate, 'shard', axis=1, tiled=True)  231 us
    all_gather x1, waiting for transfers between devices, local(): lax.all_gather(grad_work, 'shard', axis=0, tiled=True)  210 us
    all_gather x1, waiting for transfers between devices, local(): lax.all_gather(work_out, 'shard', axis=0, tiled=True)  207 us
    slice x69, local copies, waits for them, and re-layouts, recurrence(): unused, state = lax.associative_scan(combine, (carried, driven), axis=0)  178 us
  transfers between devices with their start and end apart: 16, of which 11 were waited for; matrix products, arithmetic and copies ran while one was open for 16% of the time, Pallas kernels for 0%

commit v1 on v0

v1 whole, which is shorter than its diff:
```python
import functools
from types import SimpleNamespace

import jax
import jax.numpy as jnp
from jax import lax
from jax.experimental import pallas as pl
from jax.experimental.pallas import tpu as pltpu
from jax.sharding import PartitionSpec as P

NA = 8
R = 16
NAR = NA * R
DH = 128
LIVE = 384
PLANE = 8
EPS = 1e-06
DECAY = 8.0
F32 = jnp.float32
BF16 = jnp.bfloat16
MESH_ID = pl.DeviceIdType.MESH
DMA = pltpu.SemaphoreType.DMA
ANY = pl.BlockSpec(memory_space=pl.ANY)
VM = pl.BlockSpec(memory_space=pltpu.VMEM)
VLIMIT = 60 << 20
GC = 0.7978845608028654
GA = 0.044715


def up_to(size, step):
    return -(-size // step) * step


def nn(a, b):
    return lax.dot_general(a, b, (((1,), (0,)), ((), ())), preferred_element_type=F32)


def nt(a, b):
    return lax.dot_general(a, b, (((1,), (1,)), ((), ())), preferred_element_type=F32)


def tn(a, b):
    return lax.dot_general(a, b, (((0,), (0,)), ((), ())), preferred_element_type=F32)


def gelu_parts(x):
    x2 = x * x
    th = jnp.tanh(GC * x * (1.0 + GA * x2))
    half = 0.5 * (1.0 + th)
    return x * half, half + 0.5 * x * (1.0 - th * th) * (GC * (1.0 + 3.0 * GA * x2))


def neg_expm1(x):
    series = x * (1.0 + x * (1 / 2) * (1.0 + x * (1 / 3) * (1.0 + x * (1 / 4) * (1.0 + x * (1 / 5) * (1.0 + x * (1 / 6))))))
    return jnp.where(x > -0.5, -series, 1.0 - jnp.exp(x))


class Sizes:
    def __init__(self, n, width, lru, ff, rows):
        self.n, self.d, self.rows = n, width, rows
        self.w = lru // n
        self.h = ff // n
        self.hp = up_to(self.h, 128)
        self.heads = self.w // DH
        self.cap = rows // n
        d, w, hp = width, self.w, self.hp
        self.rec = {}
        at = 0
        for name, size in (
            ("db", d), ("dg", d), ("dgates", n * w), ("dm", n * w),
            ("ub", n * w), ("ug", n * w), ("ugates", 2 * n * w), ("um", d),
        ):
            self.rec[name] = at
            at += size
        self.rec_used, self.rec_cols = at, up_to(at, 128 * PLANE)
        self.ffn = {}
        at = 0
        for name, size in (("dfg", d), ("dfu", d), ("dfd", n * hp), ("ufg", n * hp), ("ufu", n * hp), ("ufd", d)):
            self.ffn[name] = at
            at += size
        self.ffn_used, self.ffn_cols = at, up_to(at, 128 * PLANE)


def item(k, s, n):
    m = jnp.minimum(s, n - 1 - s)
    paired = k <= 2 * m
    t = jnp.where(paired, (k + 1) // 2, k - m)
    below = jnp.where(paired, k % 2 == 1, s > n - 1 - s)
    return jnp.where(below, s - t, s + t), below


def remote(src, dst, send, recv, device):
    return pltpu.make_async_remote_copy(src, dst, send, recv, device_id=device, device_id_type=MESH_ID)


def gather_kernel(n, geo, groups, *refs):
    na = len(geo)
    src, toks, sm = refs[:na], refs[na : na + 2], refs[na + 2]
    refs = refs[na + 3 :]
    dst, rtok, rsm = refs[:na], refs[na : na + 2], refs[na + 2]
    sz, sp, rz, rp, tsem, trsem = refs[na + 3 :]
    rep, s = lax.axis_index("rep"), lax.axis_index("shard")
    p = rep % PLANE

    def flip(bit):
        return rep + bit * (1 - 2 * ((rep // bit) % 2))

    def dev(r, z):
        return {"rep": r, "shard": z}

    barrier = pltpu.get_barrier_semaphore()
    for bit in (1, 2, 4):
        pl.semaphore_signal(barrier, inc=1, device_id=dev(flip(bit), s), device_id_type=MESH_ID)
    for r in range(1, n):
        pl.semaphore_signal(barrier, inc=1, device_id=dev(rep, lax.rem(s + r, n)), device_id_type=MESH_ID)
    pl.semaphore_wait(barrier, 3 + n - 1)

    def part(view, a, q):
        axis, size = geo[a]
        if axis == 0:
            return view.at[pl.ds(pl.multiple_of(q * size, 8), size)]
        return view.at[:, pl.ds(pl.multiple_of(q * size, 128), size)]

    def own(a):
        @pl.when(s < n - 1)
        def _():
            remote(part(src[a], a, p), part(dst[a].at[s], a, p), sz.at[0, a], rz.at[a, s], dev(rep, s + 1)).start()

        @pl.when(s > 0)
        def _():
            remote(part(src[a], a, p), part(dst[a].at[s], a, p), sz.at[1, a], rz.at[a, s], dev(rep, s - 1)).start()

    def own_wait(a):
        @pl.when(s < n - 1)
        def _():
            remote(part(src[a], a, p), part(dst[a].at[s], a, p), sz.at[0, a], rz.at[a, s], dev(rep, s + 1)).wait_send()

        @pl.when(s > 0)
        def _():
            remote(part(src[a], a, p), part(dst[a].at[s], a, p), sz.at[1, a], rz.at[a, s], dev(rep, s - 1)).wait_send()

    pending = []

    def plane(a, j, k, kind, q, target):
        view = part(dst[a].at[j], a, q)
        copy = remote(view, view, sp.at[kind, a, k - 1], rp.at[kind, a, j], dev(target, s))
        copy.start()
        pending.append(copy)

    def plane_wait(a, j, kind, q):
        view = part(dst[a].at[j], a, q)
        remote(view, view, sp.at[kind, a, 0], rp.at[kind, a, j], dev(rep, s)).wait_recv()

    q1, q2, q4 = p + flip(1) - rep, p + flip(2) - rep, p + flip(4) - rep
    q6 = q4 + flip(2) - rep
    q3, q5, q7 = q1 + q2 - p, q1 + q4 - p, q1 + q6 - p

    def forward(a, k):
        j, below = item(k, s, n)
        target = jnp.where(below, s + 1, s - 1)
        view = part(dst[a].at[j], a, p)
        copy = remote(view, view, sz.at[1 + k, a], rz.at[a, j], dev(rep, jnp.clip(target, 0, n - 1)))
        return (target >= 0) & (target < n), copy

    def stage1(a, k):
        j, _ = item(k, s, n)
        view = part(dst[a].at[j], a, p)
        remote(view, view, sz.at[0, a], rz.at[a, j], dev(rep, s)).wait_recv()
        valid, copy = forward(a, k)
        pl.when(valid)(copy.start)
        plane(a, j, k, 0, p, flip(2))
        plane(a, j, k, 1, p, flip(4))
        plane(a, j, k, 3, p, flip(1))

    def stage2(a, k):
        j, _ = item(k, s, n)
        plane_wait(a, j, 0, q2)
        if (a + k) % 2:
            plane(a, j, k, 2, q2, flip(4))
        plane(a, j, k, 4, q2, flip(1))
        plane_wait(a, j, 1, q4)
        if (a + k) % 2 == 0:
            plane(a, j, k, 2, q4, flip(2))
        plane(a, j, k, 5, q4, flip(1))

    def stage3(a, k):
        j, _ = item(k, s, n)
        plane_wait(a, j, 2, q6)
        plane(a, j, k, 6, q6, flip(1))

    def stage4(a, k):
        j, _ = item(k, s, n)
        for kind, q in ((3, q1), (4, q3), (5, q5), (6, q7)):
            plane_wait(a, j, kind, q)

    def line(i, view_of, into):
        copies = []
        for r in range(1, n):
            d = lax.rem(s + r, n)
            copy = remote(view_of(d), into.at[s], tsem.at[i, r], trsem.at[i, s], dev(rep, d))
            copy.start()
            copies.append(copy)
        return copies

    def line_wait(i, copies, into):
        for copy in copies:
            copy.wait_send()
        for r in range(1, n):
            d = lax.rem(s + r, n)
            remote(into.at[d], into.at[d], tsem.at[i, r], trsem.at[i, d], dev(rep, d)).wait_recv()

    items = [(a, k) for g in groups for k in range(1, n) for a in g]
    order = [a for g in groups for a in g]
    ahead, first, second = 3, len(groups[0]), len(groups[1])
    keep = pltpu.make_async_copy(sm, rsm.at[s], tsem.at[2, 0])
    keep.start()
    for a in order[:ahead]:
        own(a)
    sent = {}
    for i in range(len(items) + 6):
        if i == 3:
            sent[2] = line(2, lambda d: sm, rsm)
            sent[0] = line(0, lambda d: toks[0].at[d], rtok[0])
        if i == first * (n - 1) + 3:
            sent[1] = line(1, lambda d: toks[1].at[d], rtok[1])
        if i < len(items):
            stage1(*items[i])
        if i + ahead < first:
            own(order[i + ahead])
        m = i - (first * (n - 1) - second - ahead)
        if 0 <= m < second:
            own(groups[1][m])
        if 0 <= i - 3 < len(items):
            stage2(*items[i - 3])
        if 0 <= i - 6 < len(items):
            stage3(*items[i - 6])
    for a, k in items:
        stage4(a, k)
    line_wait(2, sent[2], rsm)
    line_wait(0, sent[0], rtok[0])
    line_wait(1, sent[1], rtok[1])
    for copy in pending:
        copy.wait_send()
    for a in order:
        own_wait(a)
    for a, k in items:
        valid, copy = forward(a, k)
        pl.when(valid)(copy.wait_send)
    keep.wait()


def gather_all(z, arrays, axes, groups, toks, sm):
    n, na = z.n, len(arrays)
    geo = [(axis, x.shape[axis] // PLANE) for x, axis in zip(arrays, axes)]
    outs = [jax.ShapeDtypeStruct((n,) + x.shape, x.dtype) for x in arrays]
    outs += [jax.ShapeDtypeStruct(t.shape, t.dtype) for t in toks]
    outs += [jax.ShapeDtypeStruct((n,) + sm.shape, sm.dtype)]
    return pl.pallas_call(
        functools.partial(gather_kernel, n, geo, groups),
        out_shape=outs,
        in_specs=[ANY] * (na + 3),
        out_specs=[ANY] * len(outs),
        scratch_shapes=[
            DMA((2 + n, na)), DMA((7, na, n - 1)), DMA((na, n)), DMA((7, na, n)), DMA((3, n)), DMA((3, n)),
        ],
        compiler_params=pltpu.CompilerParams(collective_id=1, has_side_effects=True),
        name="gather",
    )(*arrays, *toks, sm)


def start_either(s, j, own, gathered, dst, sem):
    @pl.when(j == s)
    def _():
        pltpu.make_async_copy(own, dst, sem).start()

    @pl.when(j != s)
    def _():
        pltpu.make_async_copy(gathered, dst, sem).start()


def wide(mask, width):
    return jnp.tile(mask, (1, width // 128))


def scan_rows(a_ref, x_ref, out, width, reverse):
    groups = LIVE // 8
    a = a_ref[...].reshape(groups, 8, width)
    x = x_ref[...].reshape(groups, 8, width)
    row = lax.broadcasted_iota(jnp.int32, (groups, 8, width), 1)
    for step in (1, 2, 4):
        shift = 8 - step if reverse else step
        inside = row < 8 - step if reverse else row >= step
        am = jnp.where(inside, pltpu.roll(a, shift, 1), 1.0)
        xm = jnp.where(inside, pltpu.roll(x, shift, 1), 0.0)
        x = x + a * xm
        a = a * am
    a_ref[...] = a.reshape(LIVE, width)
    x_ref[...] = x.reshape(LIVE, width)
    edge = 0 if reverse else 7

    def body(i, carry):
        g = groups - 1 - i if reverse else i
        at = pl.ds(pl.multiple_of(g * 8, 8), 8)
        value = x_ref[at, :] + a_ref[at, :] * carry
        out[at, :] = value
        return jnp.broadcast_to(value[edge : edge + 1, :], (8, width))

    lax.fori_loop(0, groups, body, jnp.zeros((8, width), F32), unroll=4)


def norm_scale(values):
    return lax.rsqrt(jnp.mean(values * values, axis=-1, keepdims=True) + EPS)


def gain_row(smv, row, n, d):
    pieces = [smv[j, row : row + 1, : d // n].astype(F32) for j in range(n)]
    return jnp.concatenate(pieces, axis=1)


def gates_of(logits, z):
    heads = z.heads
    ig = jnp.concatenate([logits[:, 2 * i * DH : (2 * i + 1) * DH] for i in range(heads)], axis=1)
    rg = jnp.concatenate([logits[:, (2 * i + 1) * DH : (2 * i + 2) * DH] for i in range(heads)], axis=1)
    return jax.nn.sigmoid(ig), jax.nn.sigmoid(rg)


def decay_of(s32, rg, first):
    soft = DECAY * jnp.log1p(jnp.exp(-s32[5:6, :]))
    log_a = -rg * soft
    a = jnp.where(first, 0.0, jnp.exp(log_a))
    scale = jnp.where(first, 1.0, jnp.sqrt(neg_expm1(2.0 * log_a)))
    return soft, a, scale


def forward_kernel(z, *refs):
    n, w, d = z.n, z.w, z.d
    (ob, og, ogw, om, oadp, otok, gb, gg, ggw, gm, gadp, gtok, sm_r, gain1, gain2, perm_r, mask_r, pos_r,
     act1_o, act2_o, resid_o, mixed_o, ranks_o, xin_o, conv_o, gi_o, ig_o, rg_o, st_o,
     wb, wg, wgw, wm, adp, tok, acc, cl, sa, sx, sem) = refs
    s = lax.axis_index("shard")
    rows = NAR // n
    waits = []

    def fetch(own, gathered, dst, sm):
        start_either(s, fetch.j, own, gathered, dst, sm)
        waits.append((own, dst, sm))

    for j in range(n):
        fetch.j = j
        fetch(otok.at[j], gtok.at[j], tok.at[pl.ds(j * z.cap, z.cap)], sem.at[0, j])
        fetch(oadp, gadp.at[j], adp.at[pl.ds(j * rows, rows)], sem.at[1, j])
    for j in range(n):
        fetch.j = j
        fetch(ob, gb.at[j], wb.at[j], sem.at[2, j])
        fetch(og, gg.at[j], wg.at[j], sem.at[3, j])
    for j in range(n):
        fetch.j = j
        fetch(ogw, ggw.at[j], wgw.at[j], sem.at[4, j])
        fetch(om, gm.at[j], wm.at[j], sem.at[5, j])
    smv, mask = sm_r, mask_r[...]
    for own, dst, sm in waits[: 2 * n]:
        pltpu.make_async_copy(own, dst, sm).wait()
    xin = nn(perm_r[...], tok[...])
    xin_o[...] = xin.astype(BF16)
    gain = gain1[...]
    act1_o[...] = (xin * norm_scale(xin) * gain).astype(BF16)
    resid_o[...] = xin
    col = z.rec

    def cols(name, size, j=0):
        return pl.ds(pl.multiple_of(col[name] + j * size, 128), size)

    ranks_o[0] = (nt(act1_o[...], adp[:, cols("db", d)]) * mask).astype(BF16)
    ranks_o[1] = (nt(act1_o[...], adp[:, cols("dg", d)]) * mask).astype(BF16)
    acc[...] = jnp.zeros_like(acc)
    for own, dst, sm in waits[2 * n : 4 * n]:
        pltpu.make_async_copy(own, dst, sm).wait()

    def first_pass(j, carry):
        s32 = smv[j].astype(F32)
        gi_o[j] = nn(act1_o[...], wg[j]) + nn(ranks_o[1], adp[:, cols("ug", w, j)])
        br = nn(act1_o[...], wb[j]) + nn(ranks_o[0], adp[:, cols("ub", w, j)])
        pos = wide(pos_r[...], w)
        total = s32[4:5, :] + s32[0:1, :] * br
        for k in range(1, 4):
            total = total + jnp.where(pos >= k, pltpu.roll(br, k, 0), 0.0) * s32[k : k + 1, :]
        conv_o[j] = total
        cl[j] = total.astype(BF16)
        acc[...] += nt(cl[j], adp[:, cols("dgates", w, j)])
        return carry

    lax.fori_loop(0, n, first_pass, 0)
    ranks_o[2] = (acc[...] * mask).astype(BF16)
    acc[...] = jnp.zeros_like(acc)
    for own, dst, sm in waits[4 * n :]:
        pltpu.make_async_copy(own, dst, sm).wait()

    def second_pass(j, carry):
        s32 = smv[j].astype(F32)
        low = cl[j]
        lift = nn(ranks_o[2], adp[:, cols("ugates", 2 * w, j)])
        bias = jnp.concatenate([s32[6:7, :], s32[7:8, :]], axis=1)
        logits = jnp.concatenate(
            [nn(low[:, i * DH : (i + 1) * DH], wgw[j, i * DH : (i + 1) * DH, :]) for i in range(z.heads)], axis=1
        ) + bias + lift
        ig, rg = gates_of(logits, z)
        first = wide(pos_r[...], w) == 0
        _, a, scale = decay_of(s32, rg, first)
        ig_o[j] = ig
        rg_o[j] = rg
        sa[...] = a
        sx[...] = scale * ig * conv_o[j]
        scan_rows(sa, sx, st_o.at[j], w, False)
        act, _ = gelu_parts(gi_o[j])
        mixed_o[j] = (st_o[j] * act).astype(BF16)
        acc[...] += nt(mixed_o[j], adp[:, cols("dm", w, j)])
        resid_o[...] += nn(mixed_o[j], wm[j])
        return carry

    lax.fori_loop(0, n, second_pass, 0)
    ranks_o[3] = (acc[...] * mask).astype(BF16)
    resid = resid_o[...] + nn(ranks_o[3], adp[:, cols("um", d)])
    resid_o[...] = resid
    act2_o[...] = (resid * norm_scale(resid) * gain2[...]).astype(BF16)


def forward_pass(z, own, gathered, tok_own, tok_all, sm, gain1, gain2, perm, mask, pos):
    n, w, d = z.n, z.w, z.d
    S = jax.ShapeDtypeStruct
    outs = [S((LIVE, d), BF16), S((LIVE, d), BF16), S((LIVE, d), F32), S((n, LIVE, w), BF16), S((4, LIVE, NAR), BF16)]
    outs += [S((LIVE, d), BF16)] + [S((n, LIVE, w), F32)] * 5
    return pl.pallas_call(
        functools.partial(forward_kernel, z),
        out_shape=outs,
        in_specs=[ANY] * 12 + [VM] * 6,
        out_specs=[VM] * len(outs),
        scratch_shapes=[
            pltpu.VMEM((n, d, w), BF16), pltpu.VMEM((n, d, w), BF16), pltpu.VMEM((n, w, 2 * DH), BF16),
            pltpu.VMEM((n, w, d), BF16), pltpu.VMEM((NAR, z.rec_cols), BF16), pltpu.VMEM((z.rows, d), BF16),
            pltpu.VMEM((LIVE, NAR), F32), pltpu.VMEM((n, LIVE, w), BF16),
            pltpu.VMEM((LIVE, w), F32), pltpu.VMEM((LIVE, w), F32), DMA((6, n)),
        ],
        compiler_params=pltpu.CompilerParams(vmem_limit_bytes=VLIMIT),
        name="forward",
    )(*own, tok_own, *gathered, tok_all, sm, gain1, gain2, perm, mask, pos)


def feed_kernel(z, *refs):
    n, d, h, hp = z.n, z.d, z.h, z.hp
    (ofg, ofu, ofd, oadp, ocot, gfg, gfu, gfd, gadp, gcot, perm_r, mask_r, gain2, act2, resid,
     out_o, gres_o, grad_o,
     wg, wu, wd, adp, tok, gl, acc_o, acc_g, rk, ra, sem, wsem) = refs
    s = lax.axis_index("shard")
    rows = NAR // n
    col = z.ffn

    def cols(name, size, j=0, stride=0):
        return pl.ds(pl.multiple_of(col[name] + j * stride, 128), size)

    for j in range(n):
        start_either(s, j, ocot.at[j], gcot.at[j], tok.at[pl.ds(j * z.cap, z.cap)], sem.at[0, j])
        start_either(s, j, oadp, gadp.at[j], adp.at[pl.ds(j * rows, rows)], sem.at[1, j])

    def load(j, slot):
        start_either(s, j, ofg, gfg.at[j], wg.at[slot], wsem.at[slot, 0])
        start_either(s, j, ofu, gfu.at[j], wu.at[slot], wsem.at[slot, 1])
        start_either(s, j, ofd, gfd.at[j], wd.at[slot], wsem.at[slot, 2])

    load(jnp.int32(0), 0)
    mask = mask_r[...]
    for j in range(n):
        pltpu.make_async_copy(ocot.at[j], tok.at[pl.ds(j * z.cap, z.cap)], sem.at[0, j]).wait()
        pltpu.make_async_copy(oadp, adp.at[pl.ds(j * rows, rows)], sem.at[1, j]).wait()
    gl[...] = nn(perm_r[...], tok[...]).astype(BF16)
    rk[0] = (nt(act2[...], adp[:, cols("dfg", d)]) * mask).astype(BF16)
    rk[1] = (nt(act2[...], adp[:, cols("dfu", d)]) * mask).astype(BF16)
    rk[2] = (nt(gl[...], adp[:, cols("ufd", d)]) * mask).astype(BF16)
    acc_o[...] = jnp.zeros_like(acc_o)
    acc_g[...] = jnp.zeros_like(acc_g)
    ra[...] = jnp.zeros_like(ra)

    def step(j, carry):
        slot = lax.rem(j, 2)
        pltpu.make_async_copy(ofg, wg.at[slot], wsem.at[slot, 0]).wait()
        pltpu.make_async_copy(ofu, wu.at[slot], wsem.at[slot, 1]).wait()
        pltpu.make_async_copy(ofd, wd.at[slot], wsem.at[slot, 2]).wait()

        @pl.when(j + 1 < n)
        def _():
            load(j + 1, 1 - slot)

        fg, fu, fd = cols("ufg", h, j, hp), cols("ufu", h, j, hp), cols("dfd", h, j, hp)
        hg = nn(act2[...], wg[slot]) + nn(rk[0], adp[:, fg])
        hu = nn(act2[...], wu[slot]) + nn(rk[1], adp[:, fu])
        gh = nt(gl[...], wd[slot]) + nn(rk[2], adp[:, fd])
        act, slope = gelu_parts(hg)
        low = (act * hu).astype(BF16)
        ghg = (gh * hu * slope).astype(BF16)
        ghu = (gh * act).astype(BF16)
        acc_o[...] += nn(low, wd[slot])
        acc_g[...] += nt(ghg, wg[slot]) + nt(ghu, wu[slot])
        ra[0] += nt(low, adp[:, fd])
        ra[1] += nt(ghg, adp[:, fg])
        ra[2] += nt(ghu, adp[:, fu])
        grad_o[:, fd] = tn(rk[2], low).astype(BF16)
        grad_o[:, fg] = tn(rk[0], ghg).astype(BF16)
        grad_o[:, fu] = tn(rk[1], ghu).astype(BF16)
        return carry

    lax.fori_loop(0, n, step, 0)
    rank = (ra[0] * mask).astype(BF16)
    work = resid[...] + acc_o[...] + nn(rank, adp[:, cols("ufd", d)])
    out_o[...] = tn(perm_r[...], work.astype(BF16)).astype(BF16)
    grad_o[:, cols("ufd", d)] = tn(rank, gl[...]).astype(BF16)
    rank_g = (ra[1] * mask).astype(BF16)
    rank_u = (ra[2] * mask).astype(BF16)
    grad_o[:, cols("dfg", d)] = tn(rank_g, act2[...]).astype(BF16)
    grad_o[:, cols("dfu", d)] = tn(rank_u, act2[...]).astype(BF16)
    gact = acc_g[...] + nn(rank_g, adp[:, cols("dfg", d)]) + nn(rank_u, adp[:, cols("dfu", d)])
    gres_o[...] = gl[...].astype(F32) + norm_back(resid[...], gact * gain2[...])


def norm_back(values, u):
    scale = norm_scale(values)
    return scale * u - values * (scale * scale * scale * jnp.mean(u * values, axis=-1, keepdims=True))


def feed_pass(z, own, gathered, cot_own, cot_all, perm, mask, gain2, act2, resid):
    n, d, h = z.n, z.d, z.h
    S = jax.ShapeDtypeStruct
    outs = [S((z.rows, d), BF16), S((LIVE, d), F32), S((NAR, z.ffn_cols), BF16)]
    return pl.pallas_call(
        functools.partial(feed_kernel, z),
        out_shape=outs,
        in_specs=[ANY] * 10 + [VM] * 5,
        out_specs=[VM] * len(outs),
        scratch_shapes=[
            pltpu.VMEM((2, d, h), BF16), pltpu.VMEM((2, d, h), BF16), pltpu.VMEM((2, h, d), BF16),
            pltpu.VMEM((NAR, z.ffn_cols), BF16), pltpu.VMEM((z.rows, d), BF16), pltpu.VMEM((LIVE, d), BF16),
            pltpu.VMEM((LIVE, d), F32), pltpu.VMEM((LIVE, d), F32),
            pltpu.VMEM((3, LIVE, NAR), BF16), pltpu.VMEM((3, LIVE, NAR), F32), DMA((2, n)), DMA((2, 3)),
        ],
        compiler_params=pltpu.CompilerParams(vmem_limit_bytes=VLIMIT),
        name="feed",
    )(*own, cot_own, *gathered, cot_all, perm, mask, gain2, act2, resid)


def backward_kernel(z, *refs):
    n, w, d = z.n, z.w, z.d
    (ob, og, ogw, om, oadp, gb, gg, ggw, gm, gadp, conv_h, gi_h, ig_h, rg_h, st_h,
     sm_r, gain1, perm_r, mask_r, pos_r, act1, mixed, ranks, xin_tok, gres,
     out_o, grad_o,
     wb, wg, wgw, wm, adp, gdir, glow, gilow, accg, acc, rk, sa, sx, st2, sav, sem, ssem) = refs
    s = lax.axis_index("shard")
    rows = NAR // n
    col = z.rec

    def cols(name, size, j=0):
        return pl.ds(pl.multiple_of(col[name] + j * size, 128), size)

    saved = (conv_h, gi_h, ig_h, rg_h, st_h)

    def load(j, slot, count=5):
        for i, ref in enumerate(saved[:count]):
            pltpu.make_async_copy(ref.at[j], sav.at[slot, i], ssem.at[slot, i]).start()

    def load_wait(j, slot, count=5):
        for i, ref in enumerate(saved[:count]):
            pltpu.make_async_copy(ref.at[j], sav.at[slot, i], ssem.at[slot, i]).wait()

    for j in range(n):
        start_either(s, j, oadp, gadp.at[j], adp.at[pl.ds(j * rows, rows)], sem.at[0, j])

    def load_merge(j, slot):
        start_either(s, j, om, gm.at[j], wm.at[slot], sem.at[1, slot])

    load_merge(jnp.int32(0), 0)
    load(0, 0)
    def load_weights(j, slot):
        start_either(s, j, ogw, ggw.at[j], wgw.at[slot], sem.at[2, slot])
        start_either(s, j, ob, gb.at[j], wb.at[slot], sem.at[3, slot])
        start_either(s, j, og, gg.at[j], wg.at[slot], sem.at[4, slot])

    load_weights(jnp.int32(0), 0)
    mask = mask_r[...]
    for j in range(n):
        pltpu.make_async_copy(oadp, adp.at[pl.ds(j * rows, rows)], sem.at[0, j]).wait()
    glm = gres[...].astype(BF16)
    rk[0] = (nt(glm, adp[:, cols("um", d)]) * mask).astype(BF16)
    grad_o[:, cols("um", d)] = tn(ranks[3], glm).astype(BF16)
    acc[...] = jnp.zeros_like(acc)

    def first_pass(j, carry):
        slot = lax.rem(j, 2)
        load_wait(j, slot)
        pltpu.make_async_copy(om, wm.at[slot], sem.at[1, slot]).wait()

        @pl.when(j + 1 < n)
        def _():
            load(j + 1, 1 - slot)
            load_merge(j + 1, 1 - slot)

        s32 = sm_r[j].astype(F32)
        conv, ig, rg, st = sav[slot, 0], sav[slot, 2], sav[slot, 3], sav[slot, 4]
        glm = gres[...].astype(BF16)
        gmix = nt(glm, wm[slot]) + nn(rk[0], adp[:, cols("dm", w, j)])
        grad_o[:, cols("dm", w, j)] = tn(rk[0], mixed[j]).astype(BF16)
        act, slope = gelu_parts(sav[slot, 1])
        gilow[j] = (gmix * st * slope).astype(BF16)
        pos = wide(pos_r[...], w)
        first = pos == 0
        soft, a, scale = decay_of(s32, rg, first)
        last = lax.broadcasted_iota(jnp.int32, (LIVE, w), 0) == LIVE - 1
        sa[...] = jnp.where(last, 0.0, pltpu.roll(a, LIVE - 1, 0))
        sx[...] = gmix * act
        scan_rows(sa, sx, st2, w, True)
        total = st2[...]
        before = jnp.where(first, 0.0, pltpu.roll(st, 1, 0))
        drive = total * scale
        gdir[j] = drive * ig
        g_in = drive * conv
        g_scale = total * ig * conv
        g_log = jnp.where(first, 0.0, total * before * a - g_scale * a * a / scale)
        g_rec = -soft * g_log
        l_in = g_in * ig * (1.0 - ig)
        l_rec = g_rec * rg * (1.0 - rg)
        pieces = []
        for i in range(z.heads):
            pieces += [l_in[:, i * DH : (i + 1) * DH], l_rec[:, i * DH : (i + 1) * DH]]
        low = jnp.concatenate(pieces, axis=1).astype(BF16)
        glow[j] = low
        acc[...] += nt(low, adp[:, cols("ugates", 2 * w, j)])
        grad_o[:, cols("ugates", 2 * w, j)] = tn(ranks[2], low).astype(BF16)
        return carry

    lax.fori_loop(0, n, first_pass, 0)
    rk[1] = (acc[...] * mask).astype(BF16)
    load(0, 0, 1)
    accg[...] = jnp.zeros_like(accg)
    rk_f = (jnp.zeros((LIVE, NAR), F32),) * 2

    def second_pass(j, carry):
        to_branch, to_gelu = carry
        slot = lax.rem(j, 2)
        load_wait(j, slot, 1)
        pltpu.make_async_copy(ogw, wgw.at[slot], sem.at[2, slot]).wait()
        pltpu.make_async_copy(ob, wb.at[slot], sem.at[3, slot]).wait()
        pltpu.make_async_copy(og, wg.at[slot], sem.at[4, slot]).wait()

        @pl.when(j + 1 < n)
        def _():
            load(j + 1, 1 - slot, 1)
            load_weights(j + 1, 1 - slot)

        s32 = sm_r[j].astype(F32)
        conv_low = sav[slot, 0].astype(BF16)
        grad_o[:, cols("dgates", w, j)] = tn(rk[1], conv_low).astype(BF16)
        low = glow[j]
        heads = jnp.concatenate(
            [nt(low[:, 2 * i * DH : 2 * (i + 1) * DH], wgw[slot, i * DH : (i + 1) * DH, :]) for i in range(z.heads)], axis=1
        )
        gconv = gdir[j] + heads + nn(rk[1], adp[:, cols("dgates", w, j)])
        pos = wide(pos_r[...], w)
        gbr = gconv * s32[0:1, :]
        for k in range(1, 4):
            gbr = gbr + pltpu.roll(jnp.where(pos >= k, gconv, 0.0), LIVE - k, 0) * s32[k : k + 1, :]
        blow = gbr.astype(BF16)
        gil = gilow[j]
        grad_o[:, cols("ub", w, j)] = tn(ranks[0], blow).astype(BF16)
        grad_o[:, cols("ug", w, j)] = tn(ranks[1], gil).astype(BF16)
        accg[...] += nt(blow, wb[slot]) + nt(gil, wg[slot])
        return (
            to_branch + nt(blow, adp[:, cols("ub", w, j)]),
            to_gelu + nt(gil, adp[:, cols("ug", w, j)]),
        )

    to_branch, to_gelu = lax.fori_loop(0, n, second_pass, rk_f)
    rank_b = (to_branch * mask).astype(BF16)
    rank_g = (to_gelu * mask).astype(BF16)
    grad_o[:, cols("db", d)] = tn(rank_b, act1[...]).astype(BF16)
    grad_o[:, cols("dg", d)] = tn(rank_g, act1[...]).astype(BF16)
    gact = accg[...] + nn(rank_b, adp[:, cols("db", d)]) + nn(rank_g, adp[:, cols("dg", d)])
    xin = xin_tok[...].astype(F32)
    gwork = gres[...] + norm_back(xin, gact * gain1[...])
    out_o[...] = tn(perm_r[...], gwork.astype(BF16)).astype(BF16)


def backward_pass(z, own, gathered, saved, sm, gain1, perm, mask, pos, act1, mixed, ranks, xin, gres):
    n, w, d = z.n, z.w, z.d
    S = jax.ShapeDtypeStruct
    V = pltpu.VMEM
    outs = [S((z.rows, d), BF16), S((NAR, z.rec_cols), BF16)]
    return pl.pallas_call(
        functools.partial(backward_kernel, z),
        out_shape=outs,
        in_specs=[ANY] * 15 + [VM] * 10,
        out_specs=[VM] * 2,
        scratch_shapes=[
            V((2, d, w), BF16), V((2, d, w), BF16), V((2, w, 2 * DH), BF16), V((2, w, d), BF16),
            V((NAR, z.rec_cols), BF16), V((n, LIVE, w), F32), V((n, LIVE, 2 * w), BF16), V((n, LIVE, w), BF16),
            V((LIVE, d), F32), V((LIVE, NAR), F32), V((2, LIVE, NAR), BF16),
            V((LIVE, w), F32), V((LIVE, w), F32), V((LIVE, w), F32), V((2, 5, LIVE, w), F32),
            DMA((5, n)), DMA((2, 5)),
        ],
        compiler_params=pltpu.CompilerParams(vmem_limit_bytes=VLIMIT),
        name="backward",
    )(*own, *gathered, *saved, sm, gain1, perm, mask, pos, act1, mixed, ranks, xin, gres)


def reduce_kernel(n, clusters, widths, *refs):
    grads, backs = refs[:2], refs[2:4]
    fins, rbacks = refs[4:6], refs[6:8]
    scratch = refs[8:]
    bufs = [SimpleNamespace(**dict(zip(("rc", "buf", "r1", "own1", "r2", "own2", "rg", "rz", "fin"), scratch[9 * t : 9 * t + 9]))) for t in range(2)]
    ssem, rsem, zs, zr, gs, gr, ps, pr, ts, tr = scratch[18:]
    rep, s = lax.axis_index("rep"), lax.axis_index("shard")
    p = rep % PLANE
    core, x, y = p % 2, (p // 2) % 2, p // 4
    rows = NAR // n
    half = NAR // 2

    def flip(bit):
        return rep + bit * (1 - 2 * ((rep // bit) % 2))

    def dev(r, place):
        return {"rep": r, "shard": place}

    barrier = pltpu.get_barrier_semaphore()
    for bit in (1, 2, 4):
        pl.semaphore_signal(barrier, inc=1, device_id=dev(flip(bit), s), device_id_type=MESH_ID)
    for r in range(1, n):
        pl.semaphore_signal(barrier, inc=1, device_id=dev(rep, lax.rem(s + r, n)), device_id_type=MESH_ID)
    for r in range(1, clusters):
        pl.semaphore_signal(barrier, inc=1, device_id=dev(lax.rem(rep + r * PLANE, clusters * PLANE), s), device_id_type=MESH_ID)
    pl.semaphore_wait(barrier, 3 + n - 1 + clusters - 1)
    pending = []

    def send(src, dst, a, b, target):
        copy = remote(src, dst, a, b, target)
        copy.start()
        pending.append(copy)

    def arrived(dst, a, b):
        remote(dst, dst, a, b, dev(rep, s)).wait_recv()

    def cut(t, q):
        return pl.ds(pl.multiple_of(q * widths[t], 128), widths[t])

    def returns(i):
        for r in range(1, n):
            d = lax.rem(s + r, n)
            send(backs[i].at[d], rbacks[i].at[s], ts.at[i, r], tr.at[i, s], dev(rep, d))

    def to_core(t):
        for c in range(4):
            send(grads[t].at[:, cut(t, 2 * c + 1 - core)], bufs[t].rc.at[c], ssem.at[t, c], rsem.at[t, c], dev(flip(1), s))

    def to_first(t):
        b = bufs[t]
        for c in range(4):
            arrived(b.rc.at[c], ssem.at[t, c], rsem.at[t, c])
            b.buf[c] = (grads[t][:, cut(t, 2 * c + core)].astype(F32) + b.rc[c].astype(F32)).astype(BF16)
        for i in range(2):
            send(b.buf.at[2 * i + 1 - x, pl.ds(0, half)], b.r1.at[0, i], ssem.at[t, 4 + i], rsem.at[t, 4 + i], dev(flip(2), s))
            send(b.buf.at[2 * (1 - y) + i, pl.ds(half, half)], b.r1.at[1, i], ssem.at[t, 6 + i], rsem.at[t, 6 + i], dev(flip(4), s))

    def to_second(t):
        b = bufs[t]
        for i in range(2):
            arrived(b.r1.at[0, i], ssem.at[t, 4 + i], rsem.at[t, 4 + i])
            b.own1[0, i] = (b.buf[2 * i + x, pl.ds(0, half)].astype(F32) + b.r1[0, i].astype(F32)).astype(BF16)
            arrived(b.r1.at[1, i], ssem.at[t, 6 + i], rsem.at[t, 6 + i])
            b.own1[1, i] = (b.buf[2 * y + i, pl.ds(half, half)].astype(F32) + b.r1[1, i].astype(F32)).astype(BF16)
        send(b.own1.at[0, 1 - y], b.r2.at[0], ssem.at[t, 8], rsem.at[t, 8], dev(flip(4), s))
        send(b.own1.at[1, 1 - x], b.r2.at[1], ssem.at[t, 9], rsem.at[t, 9], dev(flip(2), s))

    def to_line(t):
        b = bufs[t]
        arrived(b.r2.at[0], ssem.at[t, 8], rsem.at[t, 8])
        arrived(b.r2.at[1], ssem.at[t, 9], rsem.at[t, 9])
        b.own2[0, pl.ds(0, half)] = (b.own1[0, y].astype(F32) + b.r2[0].astype(F32)).astype(BF16)
        b.own2[0, pl.ds(half, half)] = (b.own1[1, x].astype(F32) + b.r2[1].astype(F32)).astype(BF16)
        if clusters > 1:
            mine = rep // PLANE
            for r in range(1, clusters):
                target = dev(lax.rem(rep + r * PLANE, clusters * PLANE), s)
                send(b.own2.at[0], b.rg.at[mine], gs.at[t, r], gr.at[t, mine], target)
            total = b.own2[0].astype(F32)
            for r in range(1, clusters):
                other = lax.rem(mine + r, clusters)
                arrived(b.rg.at[other], gs.at[t, r], gr.at[t, other])
                total = total + b.rg[other].astype(F32)
            b.own2[1] = total.astype(BF16)
        slot = 1 if clusters > 1 else 0
        for r in range(1, n):
            d = lax.rem(s + r, n)
            send(b.own2.at[slot, pl.ds(pl.multiple_of(d * rows, rows), rows)], b.rz.at[s], zs.at[t, r], zr.at[t, s], dev(rep, d))

    def to_plane(t):
        b = bufs[t]
        slot = 1 if clusters > 1 else 0
        total = b.own2[slot, pl.ds(pl.multiple_of(s * rows, rows), rows)].astype(F32)
        for r in range(1, n):
            d = lax.rem(s + r, n)
            arrived(b.rz.at[d], zs.at[t, r], zr.at[t, d])
            total = total + b.rz[d].astype(F32)
        b.fin[...] = total.astype(BF16)
        fins[t][:, cut(t, p)] = total.astype(BF16)
        spread(t, 0, p, flip(2), b.fin)
        spread(t, 1, p, flip(4), b.fin)
        spread(t, 3, p, flip(1), b.fin)

    def spread(t, kind, q, target, src=None):
        view = fins[t].at[:, cut(t, q)]
        send(view if src is None else src, view, ps.at[t, kind], pr.at[t, kind], dev(target, s))

    def spread_wait(t, kind, q):
        view = fins[t].at[:, cut(t, q)]
        arrived(view, ps.at[t, kind], pr.at[t, kind])

    q1, q2, q4 = p + flip(1) - rep, p + flip(2) - rep, p + flip(4) - rep
    q6 = q4 + flip(2) - rep
    q3, q5, q7 = q1 + q2 - p, q1 + q4 - p, q1 + q6 - p

    def across(t):
        spread_wait(t, 0, q2)
        if t == 0:
            spread(t, 2, q2, flip(4))
        spread(t, 4, q2, flip(1))
        spread_wait(t, 1, q4)
        if t == 1:
            spread(t, 2, q4, flip(2))
        spread(t, 5, q4, flip(1))

    def last(t):
        spread_wait(t, 2, q6)
        spread(t, 6, q6, flip(1))

    def end(t):
        for kind, q in ((3, q1), (4, q3), (5, q5), (6, q7)):
            spread_wait(t, kind, q)

    for i in range(2):
        returns(i)
    for step in (to_core, to_first, to_second, to_line, to_plane, across, last, end):
        for t in range(2):
            step(t)
    for i in range(2):
        for r in range(1, n):
            d = lax.rem(s + r, n)
            arrived(rbacks[i].at[d], ts.at[i, r], tr.at[i, d])
    for copy in pending:
        copy.wait_send()


def reduce_all(z, clusters, grads, backs):
    n = z.n
    rows, half = NAR // n, NAR // 2
    widths = [g.shape[1] // PLANE for g in grads]
    S = jax.ShapeDtypeStruct
    V = pltpu.VMEM
    outs = [S((rows, g.shape[1]), BF16) for g in grads] + [S(b.shape, b.dtype) for b in backs]
    scratch = []
    for c in widths:
        scratch += [
            V((4, NAR, c), BF16), V((4, NAR, c), BF16), V((2, 2, half, c), BF16), V((2, 2, half, c), BF16),
            V((2, half, c), BF16), V((2, NAR, c), BF16), V((max(clusters, 1), NAR, c), BF16), V((n, rows, c), BF16),
            V((rows, c), BF16),
        ]
    scratch += [DMA((2, 10)), DMA((2, 10)), DMA((2, n)), DMA((2, n)), DMA((2, clusters)), DMA((2, clusters)), DMA((2, 7)), DMA((2, 7)), DMA((2, n)), DMA((2, n))]
    return pl.pallas_call(
        functools.partial(reduce_kernel, n, clusters, widths),
        out_shape=outs,
        in_specs=[VM, VM, ANY, ANY],
        out_specs=[VM, VM, ANY, ANY],
        scratch_shapes=scratch,
        compiler_params=pltpu.CompilerParams(collective_id=2, has_side_effects=True, vmem_limit_bytes=VLIMIT),
        name="reduce",
    )(*grads, *backs)


def positions(lengths_row, index_row):
    ends = jnp.cumsum(lengths_row)
    starts = ends - lengths_row
    slots = jnp.arange(LIVE, dtype=jnp.int32)
    segment = jnp.sum((slots[:, None] >= ends[None, :]).astype(jnp.int32), axis=1)
    member = segment[:, None] == jnp.arange(lengths_row.shape[0], dtype=jnp.int32)[None, :]
    position = slots - jnp.sum(jnp.where(member, starts[None, :], 0), axis=1)
    chosen = jnp.sum(jnp.where(member, index_row[None, :], 0), axis=1)
    live = segment < lengths_row.shape[0]
    lanes = jnp.arange(NAR, dtype=jnp.int32) // R
    mask = ((chosen[:, None] == lanes[None, :]) & live[:, None]).astype(F32)
    return jnp.broadcast_to(position[:, None], (LIVE, NAR)), mask


def permutations(deal_row, s, n, rows):
    cap = rows // n
    deal = deal_row.reshape(n, rows)
    source = deal // rows
    slots = jnp.arange(rows, dtype=jnp.int32)
    earlier = slots[None, :] < slots[:, None]

    def rank_of(src):
        return jnp.sum((earlier[None] & (src[:, None, :] == src[:, :, None])).astype(jnp.int32), axis=2)

    rank = rank_of(source)
    mine = lax.dynamic_index_in_dim(source * cap + rank, s, 0, False)[:LIVE]
    collect = (mine[:, None] == jnp.arange(rows, dtype=jnp.int32)[None, :]).astype(BF16)
    local = deal - s * rows
    wanted = jnp.arange(cap, dtype=jnp.int32)
    hit = (source == s)[:, :, None] & (rank[:, :, None] == wanted[None, None, :])
    row = jnp.sum(jnp.where(hit, local[:, :, None], 0), axis=1).reshape(rows)
    deal_out = (row[:, None] == jnp.arange(rows, dtype=jnp.int32)[None, :]).astype(BF16)
    return collect, deal_out


def local(
    tokens, cotangent, norm_first, branch_weight, gelu_weight, conv_weight, conv_bias, gate_weight, gate_bias,
    decay_param, merge_weight, norm_second, feed_gate, feed_up, feed_down, down_branch, up_branch, down_gelu,
    up_gelu, down_gates, up_gates, down_merge, up_merge, down_feed_gate, up_feed_gate, down_feed_up, up_feed_up,
    down_feed_down, up_feed_down, seq_lengths, adapter_index, deal_order,
):
    n = lax.axis_size("shard")
    s = lax.axis_index("shard")
    clusters = lax.axis_size("rep") // PLANE
    rows, d = tokens.shape
    z = Sizes(n, d, branch_weight.shape[1] * n, feed_gate.shape[1] * n, rows)
    collect, deal_out = permutations(deal_order[0], s, n, rows)
    pos, mask = positions(seq_lengths[0], adapter_index[0])

    def send_rows(values):
        return nn(deal_out, values).astype(BF16).reshape(n, z.cap, d)

    tok_own, cot_own = send_rows(tokens), send_rows(cotangent)
    pad = z.hp - z.h

    def spaced(values):
        if pad == 0:
            return values
        parts = values.reshape(values.shape[0], n, z.h)
        return jnp.pad(parts, ((0, 0), (0, 0), (0, pad))).reshape(values.shape[0], n * z.hp)

    def packed(pieces, width):
        used = sum(x.shape[1] for x in pieces)
        pieces = list(pieces)
        if width > used:
            pieces.append(jnp.zeros((pieces[0].shape[0], width - used), BF16))
        return jnp.concatenate(pieces, axis=1)

    rec_own = packed(
        (down_branch.T, down_gelu.T, down_gates.T, down_merge.T, up_branch, up_gelu, up_gates, up_merge), z.rec_cols
    )
    ffn_own = packed(
        (down_feed_gate.T, down_feed_up.T, spaced(down_feed_down.T), spaced(up_feed_gate), spaced(up_feed_up), up_feed_down),
        z.ffn_cols,
    )
    w = z.w

    def gain(values):
        return jnp.pad(values, (0, w - values.shape[0]))[None]

    small = jnp.concatenate(
        [conv_weight, conv_bias[None], decay_param[None], gate_bias.reshape(2, w), gain(norm_first), gain(norm_second)], axis=0
    )
    small = jnp.pad(small, ((0, 16 - small.shape[0]), (0, 0)))
    gates = gate_weight.reshape(w, 2 * DH)
    arrays = [branch_weight, gelu_weight, gates, rec_own, merge_weight, feed_gate, feed_up, ffn_own, feed_down]
    axes = [0, 0, 0, 1, 0, 0, 0, 1, 0]
    got = gather_all(z, arrays, axes, [[0, 1, 2, 3, 4], [5, 6, 7, 8]], [tok_own, cot_own], small)
    branch_all, gelu_all, gates_all, rec_all, merge_all, fg_all, fu_all, ffn_all, fd_all, tok_all, cot_all, sm = got
    gain1 = sm[:, 8, : d // n].reshape(1, d).astype(F32)
    gain2 = sm[:, 9, : d // n].reshape(1, d).astype(F32)
    own = (branch_weight, gelu_weight, gates, merge_weight, rec_own)
    gathered = (branch_all, gelu_all, gates_all, merge_all, rec_all)
    act1, act2, resid, mixed, ranks, xin, *saved = forward_pass(
        z, own, gathered, tok_own, tok_all, sm, gain1, gain2, collect, mask, pos
    )
    out_send, gres, grad_ffn = feed_pass(
        z, (feed_gate, feed_up, feed_down, ffn_own), (fg_all, fu_all, fd_all, ffn_all), cot_own, cot_all,
        collect, mask, gain2, act2, resid,
    )
    tok_send, grad_rec = backward_pass(
        z, own, gathered, saved, sm, gain1, collect, mask, pos, act1, mixed, ranks, xin, gres
    )
    backs = [out_send.reshape(n, z.cap, d), tok_send.reshape(n, z.cap, d)]
    fin_ffn, fin_rec, back_out, back_tok = reduce_all(z, clusters, [grad_ffn, grad_rec], backs)

    def arrival(sent, received):
        own_block = lax.dynamic_index_in_dim(sent, s, 0, True)
        whole = lax.dynamic_update_slice_in_dim(received, own_block, s, 0)
        return tn(deal_out, whole.reshape(rows, d))

    def take(values, name, size):
        at = (z.rec if values is fin_rec else z.ffn)[name]
        return values[:, at : at + size].astype(F32)

    def unspaced(values):
        if pad == 0:
            return values
        return values.reshape(values.shape[0], n, z.hp)[:, :, : z.h].reshape(values.shape[0], n * z.h)

    lru, ffp = n * w, n * z.hp
    return (
        arrival(backs[0], back_out),
        arrival(backs[1], back_tok),
        take(fin_rec, "db", d).T,
        take(fin_rec, "ub", lru),
        take(fin_rec, "dg", d).T,
        take(fin_rec, "ug", lru),
        take(fin_rec, "dgates", lru).T,
        take(fin_rec, "ugates", 2 * lru),
        take(fin_rec, "dm", lru).T,
        take(fin_rec, "um", d),
        take(fin_ffn, "dfg", d).T,
        unspaced(take(fin_ffn, "ufg", ffp)),
        take(fin_ffn, "dfu", d).T,
        unspaced(take(fin_ffn, "ufu", ffp)),
        unspaced(take(fin_ffn, "dfd", ffp)).T,
        take(fin_ffn, "ufd", d),
    )


def solution(mesh):
    tok, line, col, row = P(("rep", "shard"), None), P("shard"), P(None, "shard"), P("shard", None)
    in_specs = (
        tok, tok, line, col, col, col, line, P("shard", None, None), row, line, row, line, col, col, row,
    ) + (col, row) * 7 + (tok, tok, P("rep", None))
    out_specs = (tok, tok) + (col, row) * 7
    return jax.shard_map(local, mesh=mesh, in_specs=in_specs, out_specs=out_specs, check_vma=False)
```

time: 3020 us -> 586 us (0.19)
  waiting for transfers between devices: 1740 us -> 0 us
  Pallas kernels: 0 us -> 538 us
  local copies, waits for them, and re-layouts: 544 us -> 14.3 us
  blocking collectives: 295 us -> 0 us
  matrix products: 234 us -> 9.94 us
  other arithmetic: 177 us -> 13.3 us
    all_gather x15 -> x0, waiting for transfers between devices: 1210 us -> none  [the longest x1 234 us: local(): lax.all_gather(feed_down, 'shard', axis=0, tiled=True)]
    pallas_call x0 -> x5, Pallas kernels: none -> 538 us  [the longest x1 288 us: gather_all(): pl.pallas_call(functools.partial(gather_kernel, n, geo, groups), out_shap...]
    psum x1 -> x0, waiting for transfers between devices: 528 us -> none  [local(): lax.psum((grad_down_branch, grad_up_branch, grad_down_gelu, grad_up_gelu,...]
    all_gather x16 -> x0, blocking collectives: 295 us -> none  [the longest x1 24.9 us: local(): lax.all_gather(down_merge, 'shard', axis=1, tiled=True)]
    pad x70 -> x3, local copies, waits for them, and re-layouts: 244 us -> 1.98 us  [the longest x2 1.37 us: gain(): return jnp.pad(values, (0, w - values.shape[0]))[None]]
    dot_general x56 -> x4, matrix products: 234 us -> 9.94 us  [the longest x2 5.55 us: tn(): lax.dot_general(a, b, (((0,), (0,)), ((), ())), preferred_element_type=F32)]
    slice x71 -> x1, local copies, waits for them, and re-layouts: 178 us -> 0.83 us  [local(): gain1 = sm[:, 8, :d // n].reshape(1, d).astype(F32)]
    mul x21 -> x0, other arithmetic: 62.9 us -> none  [the longest x15 22.1 us: combine(): return (earlier[0] * later[0], later[0] * earlier[1] + later[1])]
  transfers between devices with their start and end apart: 16 -> 0, of which waited for: 11 -> 0; matrix products, arithmetic and copies ran while one was open for 16% -> 0% of each run, Pallas kernels for 0% -> 0%
where the time goes in v1:
time: 586 us; the launch traced here: 577 us
  Pallas kernels  538 us (92%)
  local copies, waits for them, and re-layouts  14.3 us (2%)
  other arithmetic  13.3 us (2%)
  matrix products  9.94 us (2%)
    pallas_call x1, Pallas kernels, gather_all(): pl.pallas_call(functools.partial(gather_kernel, n, geo, groups), out_shap...  288 us
    pallas_call x1, Pallas kernels, reduce_all(): pl.pallas_call(functools.partial(reduce_kernel, n, clusters, widths), out...  110 us
    pallas_call x1, Pallas kernels, feed_pass(): pl.pallas_call(functools.partial(feed_kernel, z), out_shape=outs, in_spec...  62.2 us
    pallas_call x1, Pallas kernels, backward_pass(): pl.pallas_call(functools.partial(backward_kernel, z), out_shape=outs, in_...  40.6 us
    pallas_call x1, Pallas kernels, forward_pass(): pl.pallas_call(functools.partial(forward_kernel, z), out_shape=outs, in_s...  37.3 us

profile of v1, /device:TPU:0, one launch (start us, length us, event | category | flops | bytes accessed | tf_op | source)
XLA Modules:
  0.0 577.5 jit_solution(15348519658738139882)
XLA Ops:
  0.6 0.0 copy-start
  0.7 1.0 reduce-window.4
  1.7 0.7 fusion.11
  2.4 0.7 pad.11
  3.1 0.7 pad.12
  3.8 0.1 convert_reduce_fusion.1
  3.9 0.7 select_reduce_fusion.1
  4.6 0.7 broadcast_in_dim.78
  5.3 0.7 reshape.209
  6.0 0.7 broadcast_in_dim.79
  6.7 0.7 concatenate.11
  7.4 0.6 pad.13.refs_11_
  8.0 0.5 broadcast.137
  8.5 1.4 reduce.6
  9.9 0.8 broadcast_in_dim.87.refs_17_.refs_19_
  10.7 0.8 and_convert_fusion.refs_16_.refs_11_.refs_18_
  11.6 0.1 iota_compare_fusion.6
  11.7 0.0 copy-start.17
  11.7 1.2 convert_reduce_fusion
  12.9 0.0 copy-start.5
  12.9 1.1 select_reduce_fusion
  14.1 0.9 fusion.3.refs_15_.refs_10_.refs_17_
  15.1 0.0 copy-start.7
  15.2 0.0 copy-start.18
  15.3 0.7 bitcast_dynamic-update-slice_fusion.6
  16.0 0.7 bitcast_dynamic-update-slice_fusion.5
  16.6 0.7 bitcast_dynamic-update-slice_fusion
  17.4 0.7 constant_dynamic-update-slice_fusion.2
  18.1 0.7 constant_dynamic-update-slice_fusion.1
  18.9 0.6 constant_dynamic-update-slice_fusion.refs_7_.refs_3_
  19.5 2.2 convolution_convert_fusion
  21.7 2.2 convolution_convert_fusion.1
  23.9 287.9 %gather.1 = (bf16[4,1536,512]{2,1,0:T(8,128)(2,1)}, bf16[4,1536,512]{2,1,0:T(8,128)(2,1)}, bf16[4,512,256]{2,1,0:T(8,128)(2,1)}, bf16[4,32,17408]{2,1,0:T(8,128)...) custom-call(bf16[1536,512]{1,0:T(8,128)(2,1)} %refs_0_.7, ...), custom_call_target="tpu_custom_call" | custom-call | tf_op jit(solution)/shard_map/gather/pallas_call | solution.py:258
  311.8 0.8 fusion.12
  312.6 0.6 convert.10.refs_13_.refs_16_
  313.2 0.6 convert.9.refs_14_.refs_12_
  313.8 37.3 %forward.1 = (bf16[384,1536]{1,0:T(8,128)(2,1)}, bf16[384,1536]{1,0:T(8,128)(2,1)}, f32[384,1536]{1,0:T(8,128)}, bf16[4,384,512]{2,1,0:T(8,128)(2,1)}, bf16[4,38...) custom-call(bf16[1536,512]{1,0:T(8,128)(2,1)} %refs_0_.7, ...), custom_call_target="tpu_custom_call" | custom-call | tf_op jit(solution)/shard_map/forward/pallas_call | solution.py:432
  351.1 62.2 %feed.1 = (bf16[512,1536]{1,0:T(8,128)(2,1)}, f32[384,1536]{1,0:T(8,128)}, bf16[128,18432]{1,0:T(8,128)(2,1)}) custom-call(bf16[1536,1152]{1,0:T(8,128)(2,1)} %refs_0_.6, bf16[1536,1152]{1,0:T(8,128)(2,1)} %refs_1_.6, bf16[1152,1536]{1,0:T(8,128)(2,1)} %refs_2_.1, bf16[32,18432]{1,0:T(8,128)(2,1)} %constant_dynamic-update-slice_fusion.refs_7_.refs_3_, ...), custom_call_target="tpu_custom_call" | custom-call | tf_op jit(solution)/shard_map/feed/pallas_call | solution.py:532
  413.4 40.6 %backward.1 = (bf16[512,1536]{1,0:T(8,128)(2,1)}, bf16[128,17408]{1,0:T(8,128)(2,1)}) custom-call(bf16[1536,512]{1,0:T(8,128)(2,1)} %refs_0_.7, bf16[1536,512]{1,0:T(8,128)(2,1)} %refs_1_.7, bf16[512,256]{1,0:T(8,128)(2,1)} %bitcast.63, bf16[512,1536]{1,0:T(8,128)(2,1)} %refs_3_.3, bf16[32,17408]{1,0:T(8,128)(2,1)} %copy-done.2, ...), custom_call_target="tpu_custom_call" | custom-call | tf_op jit(solution)/shard_map/backward/pallas_call | solution.py:693
  454.0 110.5 %reduce.7 = (bf16[32,18432]{1,0:T(8,128)(2,1)}, bf16[32,17408]{1,0:T(8,128)(2,1)}, bf16[4,128,1536]{2,1,0:T(8,128)(2,1)}, bf16[4,128,1536]{2,1,0:T(8,128)(2,1)}) custom-call(bf16[128,18432]{1,0:T(8,128)(2,1)} %get-tuple-element.62.refs_0_, bf16[128,17408]{1,0:T(8,128)(2,1)} %get-tuple-element.73.refs_1_, bf16[4,128,1536]{2,1,0:T(8,128)(2,1)} %bitcast.57, ...), custom_call_target="tpu_custom_call" | custom-call | tf_op jit(solution)/shard_map/reduce/pallas_call | solution.py:871
  564.4 2.2 dynamic-slice_dynamic-update-slice_fusion
  566.6 0.8 slice_convert_fusion.2
  567.4 1.0 convert_bitcast_fusion.1
  568.4 1.0 slice_convert_fusion.5
  569.4 1.2 convert_bitcast_fusion
  570.7 0.8 copy-done.20
  571.5 2.8 fusion.1
  574.3 2.8 fusion
  (56 shorter events, 0.3 us)
Async XLA Ops:
  0.6 18.9 %copy-start = (bf16[512,1536]{1,0:T(8,128)(2,1)S(1)}, bf16[512,1536]{1,0:T(8,128)(2,1)}, u32[]{:S(2)}) copy-start(bf16[512,1536]{1,0:T(8,128)(2,1)} %param.32) | copy-start | bytes 4718596
  0.7 14.4 %copy-start.10 = (bf16[2048,32]{0,1:T(8,128)(2,1)S(1)}, bf16[2048,32]{0,1:T(8,128)(2,1)}, u32[]{:S(2)}) copy-start(bf16[2048,32]{0,1:T(8,128)(2,1)} %param.53) | copy-start | bytes 393220
  0.7 14.5 %copy-start.8 = (bf16[32,4096]{1,0:T(8,128)(2,1)S(1)}, bf16[32,4096]{1,0:T(8,128)(2,1)}, u32[]{:S(2)}) copy-start(bf16[32,4096]{1,0:T(8,128)(2,1)} %param.52) | copy-start | bytes 786436
  0.7 14.4 %copy-start.9 = (bf16[2048,32]{0,1:T(8,128)(2,1)S(1)}, bf16[2048,32]{0,1:T(8,128)(2,1)}, u32[]{:S(2)}) copy-start(bf16[2048,32]{0,1:T(8,128)(2,1)} %param.51) | copy-start | bytes 393220
  0.7 14.4 %copy-start.12 = (bf16[32,2048]{1,0:T(8,128)(2,1)S(1)}, bf16[32,2048]{1,0:T(8,128)(2,1)}, u32[]{:S(2)}) copy-start(bf16[32,2048]{1,0:T(8,128)(2,1)} %param.50) | copy-start | bytes 393220
  0.7 14.3 %copy-start.14 = (bf16[1536,32]{0,1:T(8,128)(2,1)S(1)}, bf16[1536,32]{0,1:T(8,128)(2,1)}, u32[]{:S(2)}) copy-start(bf16[1536,32]{0,1:T(8,128)(2,1)} %param.49) | copy-start | bytes 294916
  0.7 14.4 %copy-start.11 = (bf16[32,2048]{1,0:T(8,128)(2,1)S(1)}, bf16[32,2048]{1,0:T(8,128)(2,1)}, u32[]{:S(2)}) copy-start(bf16[32,2048]{1,0:T(8,128)(2,1)} %param.48) | copy-start | bytes 393220
  0.7 14.3 %copy-start.13 = (bf16[1536,32]{0,1:T(8,128)(2,1)S(1)}, bf16[1536,32]{0,1:T(8,128)(2,1)}, u32[]{:S(2)}) copy-start(bf16[1536,32]{0,1:T(8,128)(2,1)} %param.47) | copy-start | bytes 294916
  10.7 4.5 copy-start.15
  11.6 3.7 copy-start.16
  11.7 4.3 copy-start.17
  12.9 3.7 copy-start.5
  15.0 2.4 copy-start.6
  15.1 3.0 copy-start.7
  15.2 3.7 copy-start.18
  15.3 6.4 %copy-start.2 = (bf16[32,17408]{1,0:T(8,128)(2,1)}, bf16[32,17408]{1,0:T(8,128)(2,1)S(1)}, u32[]{:S(2)}) copy-start(bf16[32,17408]{1,0:T(8,128)(2,1)S(1)} %constant_dynamic-update-slice_fusion.3.refs_3_.refs_4_) | copy-start | bytes 3342340
  19.5 2.2 copy-start.19
  564.4 2.2 copy-start.4
  566.6 1.8 copy-start.3
  569.4 2.0 copy-start.20
  571.5 2.8 copy-start.21
  574.3 2.8 copy-start.1

commit v2 on v0

v2 whole, which is shorter than its diff:
```python
import functools

import jax
import jax.numpy as jnp
from jax import lax
from jax.experimental import pallas as pl
from jax.experimental.pallas import tpu as pltpu
from jax.sharding import PartitionSpec as P

NA = 8
R = 16
NAR = NA * R
DH = 128
LIVE = 384
PLANE = 8
EPS = 1e-06
DECAY = 8.0
F32 = jnp.float32
BF16 = jnp.bfloat16
MESH_ID = pl.DeviceIdType.MESH
DMA = pltpu.SemaphoreType.DMA
ANY = pl.BlockSpec(memory_space=pl.ANY)
VM = pl.BlockSpec(memory_space=pltpu.VMEM)
VLIMIT = 60 << 20
GC = 0.7978845608028654
GA = 0.044715


def up_to(size, step):
    return -(-size // step) * step


def nn(a, b):
    return lax.dot_general(a, b, (((1,), (0,)), ((), ())), preferred_element_type=F32)


def nt(a, b):
    return lax.dot_general(a, b, (((1,), (1,)), ((), ())), preferred_element_type=F32)


def tn(a, b):
    return lax.dot_general(a, b, (((0,), (0,)), ((), ())), preferred_element_type=F32)


def gelu_parts(x):
    x2 = x * x
    th = jnp.tanh(GC * x * (1.0 + GA * x2))
    half = 0.5 * (1.0 + th)
    return x * half, half + 0.5 * x * (1.0 - th * th) * (GC * (1.0 + 3.0 * GA * x2))


def neg_expm1(x):
    series = x * (1.0 + x * (1 / 2) * (1.0 + x * (1 / 3) * (1.0 + x * (1 / 4) * (1.0 + x * (1 / 5) * (1.0 + x * (1 / 6))))))
    return jnp.where(x > -0.5, -series, 1.0 - jnp.exp(x))


class Sizes:
    def __init__(self, n, width, lru, ff, rows):
        self.n, self.d, self.rows = n, width, rows
        self.w = lru // n
        self.h = ff // n
        self.hp = up_to(self.h, 128)
        self.heads = self.w // DH
        self.cap = rows // n
        d, w, hp = width, self.w, self.hp
        self.rec = {}
        at = 0
        for name, size in (
            ("db", d), ("dg", d), ("dgates", n * w), ("dm", n * w),
            ("ub", n * w), ("ug", n * w), ("ugates", 2 * n * w), ("um", d),
        ):
            self.rec[name] = at
            at += size
        self.rec_used, self.rec_cols = at, up_to(at, 128 * PLANE)
        self.ffn = {}
        at = 0
        for name, size in (("dfg", d), ("dfu", d), ("dfd", n * hp), ("ufg", n * hp), ("ufu", n * hp), ("ufd", d)):
            self.ffn[name] = at
            at += size
        self.ffn_used, self.ffn_cols = at, up_to(at, 128 * PLANE)


def item(k, s, n):
    m = jnp.minimum(s, n - 1 - s)
    paired = k <= 2 * m
    t = jnp.where(paired, (k + 1) // 2, k - m)
    below = jnp.where(paired, k % 2 == 1, s > n - 1 - s)
    return jnp.where(below, s - t, s + t), below


def remote(src, dst, send, recv, device):
    return pltpu.make_async_remote_copy(src, dst, send, recv, device_id=device, device_id_type=MESH_ID)


def start_either(s, j, own, gathered, dst, sem):
    @pl.when(j == s)
    def _():
        pltpu.make_async_copy(own, dst, sem).start()

    @pl.when(j != s)
    def _():
        pltpu.make_async_copy(gathered, dst, sem).start()


def wide(mask, width):
    return jnp.tile(mask, (1, width // 128))


BLOCK = 32


def scan_block(a, x, carry, reverse):
    rows, width = a.shape
    groups = rows // 8
    a, x = a.reshape(groups, 8, width), x.reshape(groups, 8, width)
    row = lax.broadcasted_iota(jnp.int32, (groups, 8, width), 1)
    for step in (1, 2, 4):
        shift = 8 - step if reverse else step
        inside = row < 8 - step if reverse else row >= step
        x = x + a * jnp.where(inside, pltpu.roll(x, shift, 1), 0.0)
        a = a * jnp.where(inside, pltpu.roll(a, shift, 1), 1.0)
    order = range(groups - 1, -1, -1) if reverse else range(groups)
    edge, far, back = (0, 7, 7) if reverse else (7, 0, 1)
    line = lax.broadcasted_iota(jnp.int32, (8, width), 0)
    values, beside = [None] * groups, [None] * groups
    for g in order:
        value = x[g] + a[g] * carry
        values[g] = value
        beside[g] = jnp.where(line == far, carry, pltpu.roll(value, back, 0))
        carry = jnp.broadcast_to(value[edge : edge + 1, :], (8, width))
    return jnp.concatenate(values, axis=0), jnp.concatenate(beside, axis=0), carry


def norm_scale(values):
    return lax.rsqrt(jnp.mean(values * values, axis=-1, keepdims=True) + EPS)


def gain_row(smv, row, n, d):
    pieces = [smv[j, row : row + 1, : d // n].astype(F32) for j in range(n)]
    return jnp.concatenate(pieces, axis=1)


def gates_of(logits, z):
    heads = z.heads
    ig = jnp.concatenate([logits[:, 2 * i * DH : (2 * i + 1) * DH] for i in range(heads)], axis=1)
    rg = jnp.concatenate([logits[:, (2 * i + 1) * DH : (2 * i + 2) * DH] for i in range(heads)], axis=1)
    return jax.nn.sigmoid(ig), jax.nn.sigmoid(rg)


def decay_of(s32, rg, first):
    soft = DECAY * jnp.log1p(jnp.exp(-s32[5:6, :]))
    log_a = -rg * soft
    a = jnp.where(first, 0.0, jnp.exp(log_a))
    scale = jnp.where(first, 1.0, jnp.sqrt(neg_expm1(2.0 * log_a)))
    return soft, a, scale


def norm_back(values, u):
    scale = norm_scale(values)
    return scale * u - values * (scale * scale * scale * jnp.mean(u * values, axis=-1, keepdims=True))


class Plane:
    def __init__(self, n):
        self.n = n
        self.rep, self.s = lax.axis_index("rep"), lax.axis_index("shard")
        self.p = p = self.rep % PLANE
        self.q1, self.q2, self.q4 = p + self.flip(1) - self.rep, p + self.flip(2) - self.rep, p + self.flip(4) - self.rep
        self.q6 = self.q4 + self.flip(2) - self.rep
        self.q3, self.q5, self.q7 = self.q1 + self.q2 - p, self.q1 + self.q4 - p, self.q1 + self.q6 - p

    def flip(self, bit):
        return self.rep + bit * (1 - 2 * ((self.rep // bit) % 2))

    def across(self, bit):
        return {"rep": self.flip(bit), "shard": self.s}

    def along(self, place):
        return {"rep": self.rep, "shard": place}

    def greet(self, clusters=1):
        barrier = pltpu.get_barrier_semaphore()
        for bit in (1, 2, 4):
            pl.semaphore_signal(barrier, inc=1, device_id=self.across(bit), device_id_type=MESH_ID)
        for r in range(1, self.n):
            pl.semaphore_signal(barrier, inc=1, device_id=self.along(lax.rem(self.s + r, self.n)), device_id_type=MESH_ID)
        for r in range(1, clusters):
            other = {"rep": lax.rem(self.rep + r * PLANE, clusters * PLANE), "shard": self.s}
            pl.semaphore_signal(barrier, inc=1, device_id=other, device_id_type=MESH_ID)
        pl.semaphore_wait(barrier, 3 + self.n - 1 + clusters - 1)


class Gather:
    def __init__(self, at, geo, src, dst, sz, sp, rz, rp):
        self.at, self.geo, self.src, self.dst = at, geo, src, dst
        self.sz, self.sp, self.rz, self.rp = sz, sp, rz, rp

    def cut(self, view, a, start, size):
        if self.geo[a][0] == 0:
            return view.at[pl.ds(pl.multiple_of(start, 8), size)]
        return view.at[:, pl.ds(pl.multiple_of(start, 128), size)]

    def part(self, view, a, q):
        size = self.geo[a][1]
        return self.cut(view, a, q * size, size)

    def got(self, a, j, q):
        return self.part(self.dst[a].at[j], a, q)

    def half(self, a, j, q, second):
        axis, size = self.geo[a]
        step = 8 if axis == 0 else 128
        first = (size // step + 1) // 2 * step
        if second:
            return self.cut(self.dst[a].at[j], a, q * size + first, size - first)
        return self.cut(self.dst[a].at[j], a, q * size, first)

    def own_copy(self, a, up):
        at = self.at
        to = at.s + 1 if up else at.s - 1
        return remote(
            self.part(self.src[a], a, at.p), self.got(a, at.s, at.p), self.sz.at[0 if up else 1, a], self.rz.at[a, at.s],
            at.along(jnp.clip(to, 0, at.n - 1)),
        )

    def own(self, a):
        pl.when(self.at.s < self.at.n - 1)(lambda: self.own_copy(a, True).start())
        pl.when(self.at.s > 0)(lambda: self.own_copy(a, False).start())

    def forward(self, a, t, up):
        at = self.at
        j = at.s - t if up else at.s + t
        to = at.s + 1 if up else at.s - 1
        came = (j >= 0) if up else (j < at.n)
        goes = (to < at.n) if up else (to >= 0)
        view = self.got(a, jnp.clip(j, 0, at.n - 1), at.p)
        sem = self.rz.at[a, jnp.clip(j, 0, at.n - 1)]
        copy = remote(view, view, self.sz.at[2 * t + (0 if up else 1), a], sem, at.along(jnp.clip(to, 0, at.n - 1)))
        return came, came & goes, copy

    def line(self, a, t):
        for up in (True, False):
            came, goes, copy = self.forward(a, t, up)
            pl.when(came)(lambda: copy.wait_recv())
            pl.when(goes)(lambda: self.forward(a, t, up)[2].start())

    def send(self, view, a, j, k, kind, bit):
        remote(view, view, self.sp.at[kind, a, k - 1], self.rp.at[kind, a, j], self.at.across(bit)).start()

    def wait(self, view, a, j, kind):
        remote(view, view, self.sp.at[kind, a, 0], self.rp.at[kind, a, j], self.at.across(1)).wait_recv()

    def place(self, k):
        return item(k, self.at.s, self.at.n)[0]

    def spread(self, a, k):
        j = self.place(k)
        view = self.got(a, j, self.at.p)
        self.send(view, a, j, k, 0, 2)
        self.send(view, a, j, k, 1, 4)
        self.send(view, a, j, k, 3, 1)

    def corner(self, a, k):
        at, j = self.at, self.place(k)
        from_x, from_y = self.got(a, j, at.q2), self.got(a, j, at.q4)
        self.wait(from_x, a, j, 0)
        self.send(self.half(a, j, at.q2, True), a, j, k, 7, 4)
        self.send(from_x, a, j, k, 4, 1)
        self.wait(from_y, a, j, 1)
        self.send(self.half(a, j, at.q4, False), a, j, k, 2, 2)
        self.send(from_y, a, j, k, 5, 1)

    def twin(self, a, k):
        at, j = self.at, self.place(k)
        self.wait(self.half(a, j, at.q6, False), a, j, 2)
        self.wait(self.half(a, j, at.q6, True), a, j, 7)
        self.send(self.got(a, j, at.q6), a, j, k, 6, 1)

    def ready(self, a, k):
        at, j = self.at, self.place(k)
        for kind, q in ((3, at.q1), (4, at.q3), (5, at.q5), (6, at.q7)):
            self.wait(self.got(a, j, q), a, j, kind)

    def drain(self):
        at = self.at
        for a in range(len(self.geo)):
            pl.when(at.s < at.n - 1)(lambda: self.own_copy(a, True).wait_send())
            pl.when(at.s > 0)(lambda: self.own_copy(a, False).wait_send())

            def body(k, carry):
                for up in (True, False):
                    _, goes, copy = self.forward(a, k, up)
                    pl.when(goes)(lambda: copy.wait_send())
                j = self.place(k)
                whole = self.got(a, j, at.p)
                for kind, view in (
                    (0, whole), (1, whole), (2, self.half(a, j, at.p, False)), (3, whole), (4, whole), (5, whole), (6, whole),
                    (7, self.half(a, j, at.p, True)),
                ):
                    remote(view, view, self.sp.at[kind, a, k - 1], self.rp.at[kind, a, j], at.across(1)).wait_send()
                return carry

            lax.fori_loop(1, at.n, body, 0)


class Line:
    def __init__(self, at, i, ssem, rsem):
        self.at, self.i, self.ssem, self.rsem = at, i, ssem, rsem

    def start(self, view_of, into, only=None):
        at = self.at
        self.into = into
        for r in range(1, at.n) if only is None else (only,):
            d = lax.rem(at.s + r, at.n)
            remote(view_of(d), into.at[at.s], self.ssem.at[self.i, r], self.rsem.at[self.i, at.s], at.along(d)).start()

    def arrived(self):
        at = self.at
        for r in range(1, at.n):
            d = lax.rem(at.s + r, at.n)
            view = self.into.at[d]
            remote(view, view, self.ssem.at[self.i, r], self.rsem.at[self.i, d], at.along(d)).wait_recv()

    def sent(self):
        view = self.into.at[0]
        for r in range(1, self.at.n):
            remote(view, view, self.ssem.at[self.i, r], self.rsem.at[self.i, 0], self.at.across(1)).wait_send()


def iota(shape, axis):
    return lax.broadcasted_iota(jnp.int32, shape, axis)


def one_hot(hit):
    return jnp.where(hit, 1.0, 0.0).astype(BF16)


def sources(deal, n, rows):
    src = jnp.zeros_like(deal)
    for k in range(1, n):
        src = src + jnp.where(deal >= k * rows, 1, 0)
    return src


def sending_order(deal_ref, s, n, rows):
    cap = rows // n
    before = one_hot(iota((rows, rows), 0) < iota((rows, rows), 1))
    deal = jnp.concatenate([deal_ref[:, b * rows : (b + 1) * rows] for b in range(n)], axis=0)
    if n < 8:
        deal = jnp.concatenate([deal, jnp.full((8 - n, rows), -1, jnp.int32)], axis=0)
    hit = (sources(deal, n, rows) == s) & (deal >= 0)
    rank = nn(one_hot(hit), before).astype(jnp.int32)
    place = jnp.where(hit, rank + iota(deal.shape, 0) * cap, -1)
    mine = deal - s * rows
    total = jnp.zeros((rows, rows), F32)
    row = iota((rows, rows), 0)
    for b in range(n):
        total = total + nt(one_hot(row == place[b : b + 1, :]), one_hot(row == mine[b : b + 1, :]))
    return total.astype(BF16)


def collecting_order(deal_ref, before, s, n, rows):
    cap = rows // n
    deal = deal_ref[:, pl.ds(pl.multiple_of(s * rows, 128), rows)]
    kind = iota((8, rows), 0)
    hit = jnp.broadcast_to(sources(deal, n, rows), (8, rows)) == kind
    rank = nn(one_hot(hit), before).astype(jnp.int32)
    place = jnp.sum(jnp.where(hit, rank + kind * cap, 0).astype(F32), axis=0, keepdims=True).astype(jnp.int32)
    return one_hot(iota((rows, LIVE), 0) == place[:, :LIVE])


def slots_of(len_ref, idx_ref, pos_ref, mask_ref):
    slot = iota((LIVE, NAR), 0)
    lane = iota((LIVE, NAR), 1)
    count = len_ref.shape[1]
    start = jnp.zeros((LIVE, NAR), jnp.int32)
    chosen = jnp.full((LIVE, NAR), idx_ref[0, 0], jnp.int32)
    end = jnp.int32(0)
    for i in range(count):
        end = end + len_ref[0, i]
        passed = slot >= end
        start = jnp.where(passed, end, start)
        chosen = jnp.where(passed, idx_ref[0, i + 1] if i + 1 < count else -1, chosen)
    pos_ref[...] = slot - start
    low = chosen * R
    mask_ref[...] = jnp.where((lane >= low) & (lane < low + R), 1.0, 0.0)


REC_PARTS = ("db", "dg", "dgates", "dm", "ub", "ug", "ugates", "um")
FFN_PARTS = ("dfg", "dfu", "dfd", "ufg", "ufu", "ufd")


def first_kernel(z, geo, *refs):
    n, w, d, h, hp = z.n, z.w, z.d, z.h, z.hp
    refs = list(refs)

    def take(count):
        out, refs[:count] = refs[:count], []
        return out

    len_r, idx_r, deal_r, small_r = take(4)
    tokens, cotangent = take(2)
    ob, og, ogw, om, ofg, ofu, ofd = take(7)
    pieces_r, pieces_f = take(8), take(6)
    gb, gg, ggw, gr, gm, gfg, gfu, gf, gfd = gathered = take(9)
    gtok, gcot, gsm = take(3)
    act1_h, xin_h, mixed_h, ranks_h, rt_h, s_h = take(6)
    conv_h, gi_h, ig_h, rg_h, st_h = take(5)
    out_h, gres_h, grad_h = take(3)
    pack_r, pack_f, rows_out, smv, s_v, rt_v, pos_r, mask_r, act1, resid, ranks = take(11)
    sz, sp, rz, rp, lss, lrs, lsem, psem, osem = take(9)
    at = Plane(n)
    s = at.s
    at.greet()
    net = Gather(at, geo, [ob, og, ogw, pack_r, om, ofg, ofu, pack_f, ofd], gathered, sz, sp, rz, rp)
    rec, ffn = [0, 1, 3, 2, 4], [5, 6, 8]
    net.own(0)
    net.own(1)
    packing = []
    for i, (dst, table, names, parts) in enumerate(((pack_r, z.rec, REC_PARTS, pieces_r), (pack_f, z.ffn, FFN_PARTS, pieces_f))):
        for k, (name, ref) in enumerate(zip(names, parts)):
            size = ref.shape[1]
            copy = pltpu.make_async_copy(ref, dst.at[:, table[name] : table[name] + size], psem.at[i, k])
            copy.start()
            packing.append(copy)
    smv[s] = small_r[...]
    lines = [Line(at, i, lss, lrs) for i in range(3)]
    lines[2].start(lambda place: small_r, gsm)
    for copy in packing:
        copy.wait()
    net.own(3)

    def sending(rows_in):
        toks = [pltpu.make_async_copy(ref, rows_in.at[i], lsem.at[0, i]) for i, ref in enumerate((tokens, cotangent))]
        for copy in toks:
            copy.start()
        order = sending_order(deal_r, s, n, z.rows)
        s_v[...] = order
        for i in range(2):
            toks[i].wait()
            rows_out[i] = nn(order, rows_in[i]).astype(BF16).reshape(n, z.cap, d)

    pl.run_scoped(sending, pltpu.VMEM((2, z.rows, d), BF16))
    before = one_hot(iota((z.rows, z.rows), 0) < iota((z.rows, z.rows), 1))
    rt_v[...] = collecting_order(deal_r, before, s, n, z.rows)
    slots_of(len_r, idx_r, pos_r, mask_r)
    outs = []

    def put(src, dst):
        copy = pltpu.make_async_copy(src, dst, osem.at[len(outs)])
        copy.start()
        outs.append(copy)

    put(s_v, s_h)
    put(rt_v, rt_h)
    put(pack_r, gr.at[s])
    put(small_r, gsm.at[s])
    items = [(a, k) for k in range(1, n) for a in rec] + [(7, k) for k in range(1, n)] + [(a, 1) for a in ffn]
    count = len(items)
    for i in range(count):
        if i in (4, 7, 10):
            for r in range(1, n):
                if (r - 1) % 3 == (4, 7, 10).index(i):
                    lines[0].start(lambda place: rows_out.at[0, place], gtok, r)
        if i >= count - 3:
            for r in range(1, n):
                if (r - 1) % 3 == i - count + 3:
                    lines[1].start(lambda place: rows_out.at[1, place], gcot, r)
        if i + 3 < len(rec):
            net.own(rec[i + 3])
        if i == len(rec):
            net.own(7)
        if 0 <= i - 9 < len(ffn):
            net.own(ffn[i - 9])
        net.line(*items[i])
        net.spread(*items[i])
        if i >= 2 and items[i - 2][0] not in ffn:
            net.corner(*items[i - 2])
        if i >= 4 and items[i - 4][0] not in ffn:
            net.twin(*items[i - 4])
    for i in range(count - 4, count):
        if items[i][0] not in ffn:
            net.twin(*items[i])
    for a, k in items:
        if a in rec:
            net.ready(a, k)
    lines[2].arrived()
    small_in = []
    for r in range(1, n):
        o = lax.rem(s + r, n)
        copy = pltpu.make_async_copy(gsm.at[o], smv.at[o], lsem.at[1, r])
        copy.start()
        small_in.append(copy)
    lines[0].arrived()
    mask = mask_r[...]

    def rows_of(i, got, into, sem):
        keep = into.at[pl.ds(pl.multiple_of(s * z.cap, 8), z.cap)]
        copies = [pltpu.make_async_copy(rows_out.at[i, s], keep, sem.at[0])]
        for r in range(1, n):
            o = lax.rem(s + r, n)
            copies.append(pltpu.make_async_copy(got.at[o], into.at[pl.ds(pl.multiple_of(o * z.cap, 8), z.cap)], sem.at[r]))
        for copy in copies:
            copy.start()
        for copy in copies:
            copy.wait()

    for copy in small_in:
        copy.wait()
    gain1, gain2 = gain_row(smv, 8, n, d), gain_row(smv, 9, n, d)

    def load_pack(pack, got, into, sem):
        rows = NAR // n
        copies = []
        for j in range(n):
            dst = into.at[pl.ds(j * rows, rows)]
            start_either(s, j, pack, got.at[j], dst, sem.at[j])
            copies.append(pltpu.make_async_copy(got.at[j], dst, sem.at[j]))
        return copies

    def recurrent(tok, wb, wg, wgw, wm, adp, conv, gi, hold, cl, mix, acc, lg, tsem, wsem, hsem):
        col = z.rec

        def cols(name, size, j=0):
            return pl.ds(pl.multiple_of(col[name] + j * size, 128), size)

        def load_a(j, slot):
            start_either(s, j, ob, gb.at[j], wb.at[slot], wsem.at[slot, 0])
            start_either(s, j, og, gg.at[j], wg.at[slot], wsem.at[slot, 1])

        def load_b(j, slot):
            start_either(s, j, ogw, ggw.at[j], wgw.at[slot], wsem.at[slot, 2])
            start_either(s, j, om, gm.at[j], wm.at[slot], wsem.at[slot, 3])

        adp_in = load_pack(pack_r, gr, adp, tsem.at[1])
        load_a(jnp.int32(0), 0)
        load_b(jnp.int32(0), 0)
        rows_of(0, gtok, tok, tsem.at[0])
        xin = tn(rt_v[...], tok[...])
        resid[...] = xin
        tok[pl.ds(0, LIVE)] = xin.astype(BF16)
        put(tok.at[pl.ds(0, LIVE)], xin_h)
        act1[...] = (xin * norm_scale(xin) * gain1).astype(BF16)
        put(act1, act1_h)
        for copy in adp_in:
            copy.wait()
        ranks[0] = (nt(act1[...], adp[:, cols("db", d)]) * mask).astype(BF16)
        ranks[1] = (nt(act1[...], adp[:, cols("dg", d)]) * mask).astype(BF16)
        acc[...] = jnp.zeros_like(acc)

        def first_pass(j, carry):
            slot = lax.rem(j, 2)
            pltpu.make_async_copy(ob, wb.at[slot], wsem.at[slot, 0]).wait()
            pltpu.make_async_copy(og, wg.at[slot], wsem.at[slot, 1]).wait()

            @pl.when(j + 1 < n)
            def _():
                load_a(j + 1, 1 - slot)

            s32 = smv[j].astype(F32)
            gi[j] = nn(act1[...], wg[slot]) + nn(ranks[1], adp[:, cols("ug", w, j)])
            lg[:, :w] = nn(act1[...], wb[slot]) + nn(ranks[0], adp[:, cols("ub", w, j)])

            def block(r, last):
                at_rows = pl.ds(pl.multiple_of(r * BLOCK, BLOCK), BLOCK)
                br = lg[at_rows, :w]
                both = jnp.concatenate([last, br], axis=0)
                pos = wide(pos_r[at_rows, :], w)
                total = s32[4:5, :] + s32[0:1, :] * br
                for k in range(1, 4):
                    total = total + jnp.where(pos >= k, both[8 - k : 8 - k + BLOCK, :], 0.0) * s32[k : k + 1, :]
                conv[j, at_rows, :] = total
                cl[j, at_rows, :] = total.astype(BF16)
                return br[BLOCK - 8 :, :]

            lax.fori_loop(0, LIVE // BLOCK, block, jnp.zeros((8, w), F32))
            pltpu.make_async_copy(conv.at[j], conv_h.at[j], hsem.at[0, j]).start()
            pltpu.make_async_copy(gi.at[j], gi_h.at[j], hsem.at[1, j]).start()
            acc[...] += nt(cl[j], adp[:, cols("dgates", w, j)])
            for i, a in enumerate(ffn):
                @pl.when(j == i + 1)
                def _():
                    if n > 2:
                        net.line(a, 2)
                    net.corner(a, 1)
            return carry

        lax.fori_loop(0, n, first_pass, 0)
        ranks[2] = (acc[...] * mask).astype(BF16)
        acc[...] = jnp.zeros_like(acc)
        holds = (ig_h, rg_h, st_h)

        def second_pass(j, carry):
            slot = lax.rem(j, 2)
            pltpu.make_async_copy(ogw, wgw.at[slot], wsem.at[slot, 2]).wait()
            pltpu.make_async_copy(om, wm.at[slot], wsem.at[slot, 3]).wait()

            @pl.when(j + 1 < n)
            def _():
                load_b(j + 1, 1 - slot)

            @pl.when(j >= 2)
            def _():
                for i, ref in enumerate(holds):
                    pltpu.make_async_copy(hold.at[slot, i], ref.at[j - 2], hsem.at[2 + i, slot]).wait()

            s32 = smv[j].astype(F32)
            low = cl[j]
            lift = nn(ranks[2], adp[:, cols("ugates", 2 * w, j)])
            bias = jnp.concatenate([s32[6:7, :], s32[7:8, :]], axis=1)
            lg[...] = jnp.concatenate(
                [nn(low[:, i * DH : (i + 1) * DH], wgw[slot, i * DH : (i + 1) * DH, :]) for i in range(z.heads)], axis=1
            ) + bias + lift

            def block(r, carry):
                at_rows = pl.ds(pl.multiple_of(r * BLOCK, BLOCK), BLOCK)
                ig, rg = gates_of(lg[at_rows, :], z)
                first = wide(pos_r[at_rows, :], w) == 0
                _, a, scale = decay_of(s32, rg, first)
                hold[slot, 0, at_rows, :] = ig
                hold[slot, 1, at_rows, :] = rg
                state, _, carry = scan_block(a, scale * ig * conv[j, at_rows, :], carry, False)
                hold[slot, 2, at_rows, :] = state
                act, _ = gelu_parts(gi[j, at_rows, :])
                mix[j, at_rows, :] = (state * act).astype(BF16)
                return carry

            lax.fori_loop(0, LIVE // BLOCK, block, jnp.zeros((8, w), F32))
            for i, ref in enumerate(holds):
                pltpu.make_async_copy(hold.at[slot, i], ref.at[j], hsem.at[2 + i, slot]).start()
            acc[...] += nt(mix[j], adp[:, cols("dm", w, j)])
            resid[...] += nn(mix[j], wm[slot])
            for i, a in enumerate(ffn):
                @pl.when(j == i)
                def _():
                    if n > 2:
                        net.spread(a, 2)
                    if n > 3:
                        net.line(a, 3)
            return carry

        lax.fori_loop(0, n, second_pass, 0)
        put(mix, mixed_h)
        ranks[3] = (acc[...] * mask).astype(BF16)
        put(ranks, ranks_h)
        resid[...] = resid[...] + nn(ranks[3], adp[:, cols("um", d)])
        for j in range(n):
            pltpu.make_async_copy(conv.at[j], conv_h.at[j], hsem.at[0, j]).wait()
            pltpu.make_async_copy(gi.at[j], gi_h.at[j], hsem.at[1, j]).wait()
        for j in (n - 2, n - 1):
            for i, ref in enumerate(holds):
                pltpu.make_async_copy(hold.at[j % 2, i], ref.at[j], hsem.at[2 + i, j % 2]).wait()
        for copy in outs[4:]:
            copy.wait()

    V = pltpu.VMEM
    pl.run_scoped(
        recurrent,
        V((z.rows, d), BF16), V((2, d, w), BF16), V((2, d, w), BF16), V((2, w, 2 * DH), BF16), V((2, w, d), BF16),
        V((NAR, z.rec_cols), BF16), V((n, LIVE, w), F32), V((n, LIVE, w), F32), V((2, 3, LIVE, w), F32),
        V((n, LIVE, w), BF16), V((n, LIVE, w), BF16), V((LIVE, NAR), F32), V((LIVE, 2 * w), F32),
        DMA((2, n)), DMA((2, 4)), DMA((5, n)),
    )

    def feed(tok, wg, wu, wd, adp, act2, gl, acc_o, acc_g, rk, ra, grad_o, hgs, hus, ghs, low, ghg, ghu, tsem, wsem):
        col = z.ffn

        def cols(name, size, j=0, stride=0):
            return pl.ds(pl.multiple_of(col[name] + j * stride, 128), size)

        base = resid[...]
        act2[...] = (base * norm_scale(base) * gain2).astype(BF16)
        acc_o[...] = jnp.zeros_like(acc_o)
        acc_g[...] = jnp.zeros_like(acc_g)
        ra[...] = jnp.zeros_like(ra)
        weights = ((5, ofg, gfg, wg), (6, ofu, gfu, wu), (8, ofd, gfd, wd))
        for k in range(1, n):
            net.ready(7, k)
        lines[1].arrived()
        rows_of(1, gcot, tok, tsem.at[0])
        gl[...] = tn(rt_v[...], tok[...]).astype(BF16)

        def tick(i, q):
            a = ffn[i]

            @pl.when(q + 3 < n)
            def _():
                net.spread(a, q + 3)

            @pl.when(q + 4 < n)
            def _():
                net.line(a, q + 4)

            @pl.when(q + 2 < n)
            def _():
                net.corner(a, q + 2)

            @pl.when(q + 1 < n)
            def _():
                net.twin(a, q + 1)

        def step(q, carry):
            j = jnp.where(q == 0, s, item(jnp.maximum(q, 1), s, n)[0])
            for i, (a, mine, got, into) in enumerate(weights):
                @pl.when(q > 0)
                def _():
                    net.ready(a, q)
                    pltpu.make_async_copy(got.at[j], into, wsem.at[i]).start()

            fg, fu, fd = cols("ufg", h, j, hp), cols("ufu", h, j, hp), cols("dfd", h, j, hp)
            pltpu.make_async_copy(ofg, wg, wsem.at[0]).wait()
            hgs[...] = nn(act2[...], wg[...]) + nn(rk[0], adp[:, fg])
            pltpu.make_async_copy(ofu, wu, wsem.at[1]).wait()
            hus[...] = nn(act2[...], wu[...]) + nn(rk[1], adp[:, fu])
            tick(0, q)
            pltpu.make_async_copy(ofd, wd, wsem.at[2]).wait()
            ghs[...] = nt(gl[...], wd[...]) + nn(rk[2], adp[:, fd])

            def block(r, carry):
                at_rows = pl.ds(pl.multiple_of(r * 16, 16), 16)
                act, slope = gelu_parts(hgs[at_rows, :])
                hu, gh = hus[at_rows, :], ghs[at_rows, :]
                low[at_rows, :] = (act * hu).astype(BF16)
                ghg[at_rows, :] = (gh * hu * slope).astype(BF16)
                ghu[at_rows, :] = (gh * act).astype(BF16)
                return carry

            lax.fori_loop(0, LIVE // 16, block, 0)
            tick(1, q)
            acc_o[...] += nn(low[...], wd[...])
            ra[0] += nt(low[...], adp[:, fd])
            ra[1] += nt(ghg[...], adp[:, fg])
            ra[2] += nt(ghu[...], adp[:, fu])
            tick(2, q)
            acc_g[...] += nt(ghg[...], wg[...]) + nt(ghu[...], wu[...])
            grad_o[:, fd] = tn(rk[2], low[...]).astype(BF16)
            grad_o[:, fg] = tn(rk[0], ghg[...]).astype(BF16)
            grad_o[:, fu] = tn(rk[1], ghu[...]).astype(BF16)
            return carry

        adp_in = load_pack(pack_f, gf, adp, tsem.at[1])
        for i, (a, mine, got, into) in enumerate(weights):
            pltpu.make_async_copy(mine, into, wsem.at[i]).start()
        for copy in adp_in:
            copy.wait()
        rk[0] = (nt(act2[...], adp[:, cols("dfg", d)]) * mask).astype(BF16)
        rk[1] = (nt(act2[...], adp[:, cols("dfu", d)]) * mask).astype(BF16)
        rk[2] = (nt(gl[...], adp[:, cols("ufd", d)]) * mask).astype(BF16)
        lax.fori_loop(0, n, step, 0)
        rank = (ra[0] * mask).astype(BF16)
        work = resid[...] + acc_o[...] + nn(rank, adp[:, cols("ufd", d)])
        tok[...] = nn(rt_v[...], work.astype(BF16)).astype(BF16)
        put(tok, out_h)
        grad_o[:, cols("ufd", d)] = tn(rank, gl[...]).astype(BF16)
        rank_g = (ra[1] * mask).astype(BF16)
        rank_u = (ra[2] * mask).astype(BF16)
        grad_o[:, cols("dfg", d)] = tn(rank_g, act2[...]).astype(BF16)
        grad_o[:, cols("dfu", d)] = tn(rank_u, act2[...]).astype(BF16)
        gact = acc_g[...] + nn(rank_g, adp[:, cols("dfg", d)]) + nn(rank_u, adp[:, cols("dfu", d)])
        put(grad_o, grad_h)
        resid[...] = gl[...].astype(F32) + norm_back(resid[...], gact * gain2)
        put(resid, gres_h)
        for copy in outs[8:]:
            copy.wait()

    pl.run_scoped(
        feed,
        V((z.rows, d), BF16), V((d, h), BF16), V((d, h), BF16), V((h, d), BF16), V((NAR, z.ffn_cols), BF16),
        V((LIVE, d), BF16), V((LIVE, d), BF16), V((LIVE, d), F32), V((LIVE, d), F32),
        V((3, LIVE, NAR), BF16), V((3, LIVE, NAR), F32), V((NAR, z.ffn_cols), BF16),
        V((LIVE, h), F32), V((LIVE, h), F32), V((LIVE, h), F32), V((LIVE, h), BF16), V((LIVE, h), BF16), V((LIVE, h), BF16),
        DMA((2, n)), DMA((3,)),
    )
    for line in lines:
        line.sent()
    for copy in outs[:4]:
        copy.wait()
    net.drain()


def run_first(z, geo, *args):
    n, w, d = z.n, z.w, z.d
    S, V = jax.ShapeDtypeStruct, pltpu.VMEM
    sources_ = args[6:13]
    shapes = [sources_[0], sources_[1], sources_[2], (NAR // n, z.rec_cols), sources_[3], sources_[4], sources_[5], (NAR // n, z.ffn_cols), sources_[6]]
    outs = [S((n,) + tuple(x.shape if hasattr(x, "shape") else x), BF16) for x in shapes]
    na = len(outs)
    outs += [S((n, z.cap, d), BF16)] * 2 + [S((n, 16, w), BF16)]
    outs += [S((LIVE, d), BF16), S((LIVE, d), BF16), S((n, LIVE, w), BF16), S((4, LIVE, NAR), BF16), S((z.rows, LIVE), BF16), S((z.rows, z.rows), BF16)]
    outs += [S((n, LIVE, w), F32)] * 5
    outs += [S((z.rows, d), BF16), S((LIVE, d), F32), S((NAR, z.ffn_cols), BF16)]
    SM = pl.BlockSpec(memory_space=pltpu.SMEM)
    return pl.pallas_call(
        functools.partial(first_kernel, z, geo),
        out_shape=outs,
        in_specs=[SM, SM, VM, VM] + [ANY] * (len(args) - 4),
        out_specs=[ANY] * len(outs),
        scratch_shapes=[
            V((NAR // n, z.rec_cols), BF16), V((NAR // n, z.ffn_cols), BF16), V((2, n, z.cap, d), BF16), V((n, 16, w), BF16),
            V((z.rows, z.rows), BF16), V((z.rows, LIVE), BF16), V((LIVE, NAR), jnp.int32), V((LIVE, NAR), F32),
            V((LIVE, d), BF16), V((LIVE, d), F32), V((4, LIVE, NAR), BF16),
            DMA((2 * n, na)), DMA((8, na, n - 1)), DMA((na, n)), DMA((8, na, n)), DMA((3, n)), DMA((3, n)),
            DMA((2, n)), DMA((2, 8)), DMA((11,)),
        ],
        compiler_params=pltpu.CompilerParams(collective_id=1, has_side_effects=True, vmem_limit_bytes=VLIMIT),
        name="first",
    )(*args)


def add_rows(dst, left, right, rows, step=16):
    def body(r, carry):
        at_rows = pl.ds(pl.multiple_of(r * step, step), step)
        dst[at_rows, :] = (left[at_rows, :].astype(F32) + right[at_rows, :].astype(F32)).astype(BF16)
        return carry

    lax.fori_loop(0, rows // step, body, 0)


class Reduce:
    def __init__(self, at, t, clusters, width, source, own, fin, bufs, sems):
        self.at, self.t, self.clusters, self.c = at, t, clusters, width
        self.source, self.own, self.fin = source, own, fin
        self.rc, self.r1, self.r2, self.rg, self.rz, self.sm = bufs
        self.ss, self.rs, self.zs, self.zr, self.gs, self.gr, self.ps, self.pr = [x.at[t] for x in sems]
        p = at.p
        self.core, self.x, self.y = p % 2, (p // 2) % 2, p // 4
        self.rows, self.half = NAR // at.n, NAR // 2

    def cut(self, q):
        return pl.ds(pl.multiple_of(q * self.c, 128), self.c)

    def send(self, src, dst, a, b, device):
        remote(src, dst, a, b, device).start()

    def arrived(self, dst, a, b):
        remote(dst, dst, a, b, self.at.across(1)).wait_recv()

    def to_core(self):
        for c in range(4):
            self.send(self.source.at[:, self.cut(2 * c + 1 - self.core)], self.rc.at[c], self.ss.at[c], self.rs.at[c], self.at.across(1))

    def to_first(self):
        for c in range(4):
            self.arrived(self.rc.at[c], self.ss.at[c], self.rs.at[c])
            add_rows(self.rc.at[c], self.own(c), self.rc.at[c], NAR)
        low, high = pl.ds(0, self.half), pl.ds(self.half, self.half)
        for i in range(2):
            self.send(self.rc.at[2 * i + 1 - self.x, low], self.r1.at[0, i], self.ss.at[4 + i], self.rs.at[4 + i], self.at.across(2))
            self.send(self.rc.at[2 * (1 - self.y) + i, high], self.r1.at[1, i], self.ss.at[6 + i], self.rs.at[6 + i], self.at.across(4))

    def to_second(self):
        low, high = pl.ds(0, self.half), pl.ds(self.half, self.half)
        for i in range(2):
            self.arrived(self.r1.at[0, i], self.ss.at[4 + i], self.rs.at[4 + i])
            add_rows(self.r1.at[0, i], self.rc.at[2 * i + self.x, low], self.r1.at[0, i], self.half)
            self.arrived(self.r1.at[1, i], self.ss.at[6 + i], self.rs.at[6 + i])
            add_rows(self.r1.at[1, i], self.rc.at[2 * self.y + i, high], self.r1.at[1, i], self.half)
        self.send(self.r1.at[0, 1 - self.y], self.r2.at[0, low], self.ss.at[8], self.rs.at[8], self.at.across(4))
        self.send(self.r1.at[1, 1 - self.x], self.r2.at[0, high], self.ss.at[9], self.rs.at[9], self.at.across(2))

    def to_line(self):
        at = self.at
        low, high = pl.ds(0, self.half), pl.ds(self.half, self.half)
        self.arrived(self.r2.at[0, low], self.ss.at[8], self.rs.at[8])
        add_rows(self.r2.at[0, low], self.r1.at[0, self.y], self.r2.at[0, low], self.half)
        self.arrived(self.r2.at[0, high], self.ss.at[9], self.rs.at[9])
        add_rows(self.r2.at[0, high], self.r1.at[1, self.x], self.r2.at[0, high], self.half)
        if self.clusters > 1:
            mine = at.rep // PLANE
            for r in range(1, self.clusters):
                device = {"rep": lax.rem(at.rep + r * PLANE, self.clusters * PLANE), "shard": at.s}
                self.send(self.r2.at[0], self.rg.at[mine], self.gs.at[r], self.gr.at[mine], device)
            self.rg[mine] = self.r2[0]
            for r in range(1, self.clusters):
                other = lax.rem(mine + r, self.clusters)
                self.arrived(self.rg.at[other], self.gs.at[r], self.gr.at[other])
            add_rows(self.r2.at[1], self.rg.at[0], self.rg.at[1], NAR)
            for other in range(2, self.clusters):
                add_rows(self.r2.at[1], self.rg.at[other], self.r2.at[1], NAR)
        self.final = 1 if self.clusters > 1 else 0
        for r in range(1, at.n):
            d = lax.rem(at.s + r, at.n)
            chunk = pl.ds(pl.multiple_of(d * self.rows, self.rows), self.rows)
            self.send(self.r2.at[self.final, chunk], self.rz.at[at.s], self.zs.at[r], self.zr.at[at.s], at.along(d))

    def to_plane(self):
        at = self.at
        total = self.r2[self.final, pl.ds(pl.multiple_of(at.s * self.rows, self.rows), self.rows), :].astype(F32)
        for r in range(1, at.n):
            d = lax.rem(at.s + r, at.n)
            self.arrived(self.rz.at[d], self.zs.at[r], self.zr.at[d])
            total = total + self.rz[d].astype(F32)
        self.sm[...] = total.astype(BF16)
        self.fin[:, self.cut(at.p)] = total.astype(BF16)
        for kind, bit in ((0, 2), (1, 4), (3, 1)):
            self.spread(kind, at.p, bit, self.sm)

    def spread(self, kind, q, bit, src=None):
        view = self.fin.at[:, self.cut(q)]
        self.send(view if src is None else src, view, self.ps.at[kind], self.pr.at[kind], self.at.across(bit))

    def spread_wait(self, kind, q):
        self.arrived(self.fin.at[:, self.cut(q)], self.ps.at[kind], self.pr.at[kind])

    def over(self):
        at = self.at
        self.spread_wait(0, at.q2)
        if self.t % 2 == 0:
            self.spread(2, at.q2, 4)
        self.spread(4, at.q2, 1)
        self.spread_wait(1, at.q4)
        if self.t % 2 == 1:
            self.spread(2, at.q4, 2)
        self.spread(5, at.q4, 1)

    def last(self):
        self.spread_wait(2, self.at.q6)
        self.spread(6, self.at.q6, 1)

    def end(self):
        at = self.at
        for kind, q in ((3, at.q1), (4, at.q3), (5, at.q5), (6, at.q7)):
            self.spread_wait(kind, q)
        sent = [(self.rc.at[0], self.ss.at[c]) for c in range(4)]
        sent += [(self.r1.at[0, 0], self.ss.at[4 + i]) for i in range(4)]
        sent += [(self.r2.at[0, pl.ds(0, self.half)], self.ss.at[8 + i]) for i in range(2)]
        sent += [(self.rg.at[0], self.gs.at[r]) for r in range(1, self.clusters)]
        sent += [(self.rz.at[0], self.zs.at[r]) for r in range(1, at.n)]
        sent += [(self.sm, self.ps.at[kind]) for kind in range(7)]
        for view, sem in sent:
            remote(view, view, sem, sem, at.across(1)).wait_send()


def early_table(z):
    return {"um": 0, "dm": z.d, "ugates": z.d + z.n * z.w}, up_to(z.d + 3 * z.n * z.w, 128 * PLANE)


def late_table(z):
    lru = z.n * z.w
    return {"dgates": 0, "ub": lru, "ug": 2 * lru, "db": 3 * lru, "dg": 3 * lru + z.d}, up_to(3 * lru + 2 * z.d, 128 * PLANE)


def second_kernel(z, clusters, *refs):
    n, w, d = z.n, z.w, z.d
    refs = list(refs)

    def take(count):
        out, refs[:count] = refs[:count], []
        return out

    len_r, idx_r, rt_v, gres, ranks = take(5)
    sm_h, ob, og, ogw, om, gb, gg, ggw, gm, gr = take(10)
    conv_h, gi_h, ig_h, rg_h, st_h, act1_h, xin_h, mixed_h, out_h, gradf_h = take(10)
    back_out, back_tok, fin_f, fin_e, fin_l = take(5)
    pos_r, mask_r, smv, adp, glm, gdir, glow, gilow, gmix, acc, rk, accg, tokv, grad_e, grad_l, own_f = take(16)
    bufs = [take(6) for _ in range(3)]
    sems = take(8)
    lss, lrs, lsem = take(3)
    at = Plane(n)
    s = at.s
    at.greet(clusters)
    lines = [Line(at, i, lss, lrs) for i in range(2)]
    lines[0].start(lambda place: out_h.at[place], back_out)
    keep = pltpu.make_async_copy(out_h.at[s], back_out.at[s], lsem.at[0, 0])
    keep.start()
    (early, _), (late, _) = early_table(z), late_table(z)
    core = at.p % 2

    def own_of(ref, width):
        return lambda c: ref.at[:, pl.ds(pl.multiple_of((2 * c + core) * width, 128), width)]

    widths = [x.shape[2] for x in (bufs[0][0], bufs[1][0], bufs[2][0])]
    red_f = Reduce(at, 0, clusters, widths[0], gradf_h, lambda c: own_f.at[c], fin_f, bufs[0], sems)
    red_e = Reduce(at, 1, clusters, widths[1], grad_e, own_of(grad_e, widths[1]), fin_e, bufs[1], sems)
    red_l = Reduce(at, 2, clusters, widths[2], grad_l, own_of(grad_l, widths[2]), fin_l, bufs[2], sems)
    red_f.to_core()
    rows = NAR // n
    own_in = [pltpu.make_async_copy(own_of(gradf_h, widths[0])(c), own_f.at[c], lsem.at[1, c]) for c in range(4)]
    packs = [pltpu.make_async_copy(gr.at[j], adp.at[pl.ds(j * rows, rows)], lsem.at[2, j]) for j in range(n)]
    small_in = pltpu.make_async_copy(sm_h, smv, lsem.at[0, 1])
    for copy in own_in + packs + [small_in]:
        copy.start()
    slots_of(len_r, idx_r, pos_r, mask_r)
    mask = mask_r[...]
    col = z.rec

    def cols(name, size, j=0):
        return pl.ds(pl.multiple_of(col[name] + j * size, 128), size)

    def put_at(table, name, size, j=0):
        return pl.ds(pl.multiple_of(table[name] + j * size, 128), size)

    def rows_at(r):
        return pl.ds(pl.multiple_of(r * BLOCK, BLOCK), BLOCK)

    blocks = LIVE // BLOCK

    def state_pass(sav, wm, mixed, ssem):
        saved = (conv_h, gi_h, ig_h, rg_h, st_h)

        def load(j, slot):
            start_either(s, j, om, gm.at[j], wm.at[slot], ssem.at[slot, 5])
            for i, ref in enumerate(saved):
                pltpu.make_async_copy(ref.at[j], sav.at[slot, i], ssem.at[slot, i]).start()
            pltpu.make_async_copy(mixed_h.at[j], mixed.at[slot], ssem.at[slot, 6]).start()

        def load_wait(slot):
            pltpu.make_async_copy(om, wm.at[slot], ssem.at[slot, 5]).wait()
            for i, ref in enumerate(saved):
                pltpu.make_async_copy(ref.at[0], sav.at[slot, i], ssem.at[slot, i]).wait()
            pltpu.make_async_copy(mixed_h.at[0], mixed.at[slot], ssem.at[slot, 6]).wait()

        load(jnp.int32(0), 0)
        glm[...] = gres[...].astype(BF16)
        for copy in packs + [small_in]:
            copy.wait()
        rk[0] = (nt(glm[...], adp[:, cols("um", d)]) * mask).astype(BF16)
        grad_e[:, put_at(early, "um", d)] = tn(ranks[3], glm[...]).astype(BF16)
        acc[...] = jnp.zeros_like(acc)
        for copy in own_in:
            copy.wait()
        red_f.to_first()

        def body(j, carry):
            slot = lax.rem(j, 2)
            load_wait(slot)

            @pl.when(j + 1 < n)
            def _():
                load(j + 1, 1 - slot)

            s32 = smv[j].astype(F32)
            gmix[...] = nt(glm[...], wm[slot]) + nn(rk[0], adp[:, cols("dm", w, j)])
            grad_e[:, put_at(early, "dm", w, j)] = tn(rk[0], mixed[slot]).astype(BF16)

            def block(i, carry):
                at_rows = rows_at(blocks - 1 - i)
                gmx, conv, ig = gmix[at_rows, :], sav[slot, 0, at_rows, :], sav[slot, 2, at_rows, :]
                rg, state = sav[slot, 3, at_rows, :], sav[slot, 4, at_rows, :]
                act, slope = gelu_parts(sav[slot, 1, at_rows, :])
                gilow[j, at_rows, :] = (gmx * state * slope).astype(BF16)
                first = wide(pos_r[at_rows, :], w) == 0
                soft, a, scale = decay_of(s32, rg, first)
                x = gmx * act
                _, after, carry = scan_block(a, a * x, carry, True)
                total = x + after
                drive = total * scale
                gdir[j, at_rows, :] = drive * ig
                fed = ig * conv
                kept = total * (state - scale * fed)
                g_log = jnp.where(first, 0.0, kept - total * fed * (a * a) / scale)
                l_in = drive * conv * ig * (1.0 - ig)
                l_rec = -soft * g_log * rg * (1.0 - rg)
                for i in range(z.heads):
                    glow[j, at_rows, 2 * i * DH : (2 * i + 1) * DH] = l_in[:, i * DH : (i + 1) * DH].astype(BF16)
                    glow[j, at_rows, (2 * i + 1) * DH : (2 * i + 2) * DH] = l_rec[:, i * DH : (i + 1) * DH].astype(BF16)
                return carry

            lax.fori_loop(0, blocks, block, jnp.zeros((8, w), F32))
            acc[...] += nt(glow[j], adp[:, cols("ugates", 2 * w, j)])
            grad_e[:, put_at(early, "ugates", 2 * w, j)] = tn(ranks[2], glow[j]).astype(BF16)
            return carry

        lax.fori_loop(0, n, body, 0)

    V = pltpu.VMEM
    pl.run_scoped(state_pass, V((2, 5, LIVE, w), F32), V((2, w, d), BF16), V((2, LIVE, w), BF16), DMA((2, 7)))
    rk[1] = (acc[...] * mask).astype(BF16)
    red_e.to_core()

    def branch_pass(wb, wg, wgw, conv, blow, act1, xin, grads_rank, wsem, asem):
        def load(j, slot):
            start_either(s, j, ob, gb.at[j], wb.at[slot], wsem.at[slot, 0])
            start_either(s, j, og, gg.at[j], wg.at[slot], wsem.at[slot, 1])
            start_either(s, j, ogw, ggw.at[j], wgw.at[slot], wsem.at[slot, 2])
            pltpu.make_async_copy(conv_h.at[j], conv.at[slot], wsem.at[slot, 3]).start()

        ends = [pltpu.make_async_copy(act1_h, act1, asem.at[0]), pltpu.make_async_copy(xin_h, xin, asem.at[1])]
        load(jnp.int32(0), 0)
        for copy in ends:
            copy.start()
        red_f.to_second()
        accg[...] = jnp.zeros_like(accg)
        grads_rank[...] = jnp.zeros_like(grads_rank)

        def body(j, carry):
            slot = lax.rem(j, 2)
            for i, (ref, into) in enumerate(((ob, wb), (og, wg), (ogw, wgw), (conv_h.at[0], conv))):
                pltpu.make_async_copy(ref, into.at[slot], wsem.at[slot, i]).wait()

            @pl.when(j + 1 < n)
            def _():
                load(j + 1, 1 - slot)

            s32 = smv[j].astype(F32)
            grad_l[:, put_at(late, "dgates", w, j)] = tn(rk[1], conv[slot].astype(BF16)).astype(BF16)
            low = glow[j]
            heads = jnp.concatenate(
                [nt(low[:, 2 * i * DH : 2 * (i + 1) * DH], wgw[slot, i * DH : (i + 1) * DH, :]) for i in range(z.heads)], axis=1
            )
            gmix[...] = gdir[j] + heads + nn(rk[1], adp[:, cols("dgates", w, j)])

            def block(i, carry):
                later, later_pos = carry
                at_rows = rows_at(blocks - 1 - i)
                cur, pos = gmix[at_rows, :], pos_r[at_rows, :]
                both = jnp.concatenate([cur, later], axis=0)
                both_pos = jnp.concatenate([pos, later_pos], axis=0)
                total = cur * s32[0:1, :]
                for k in range(1, 4):
                    inside = wide(both_pos[k : k + BLOCK, :], w) >= k
                    total = total + jnp.where(inside, both[k : k + BLOCK, :], 0.0) * s32[k : k + 1, :]
                blow[at_rows, :] = total.astype(BF16)
                return cur[:8, :], pos[:8, :]

            lax.fori_loop(0, blocks, block, (jnp.zeros((8, w), F32), jnp.zeros((8, NAR), jnp.int32)))
            gil = gilow[j]
            grad_l[:, put_at(late, "ub", w, j)] = tn(ranks[0], blow[...]).astype(BF16)
            grad_l[:, put_at(late, "ug", w, j)] = tn(ranks[1], gil).astype(BF16)
            accg[...] += nt(blow[...], wb[slot]) + nt(gil, wg[slot])
            grads_rank[0] += nt(blow[...], adp[:, cols("ub", w, j)])
            grads_rank[1] += nt(gil, adp[:, cols("ug", w, j)])
            pl.when(j == 0)(red_e.to_first)
            pl.when(j == n - 1)(red_f.to_line)
            return carry

        lax.fori_loop(0, n, body, 0)
        rank_b = (grads_rank[0] * mask).astype(BF16)
        rank_g = (grads_rank[1] * mask).astype(BF16)
        for copy in ends:
            copy.wait()
        gain1 = gain_row(smv, 8, n, d)
        gact = accg[...] + nn(rank_b, adp[:, cols("db", d)]) + nn(rank_g, adp[:, cols("dg", d)])
        gwork = gres[...] + norm_back(xin[...].astype(F32), gact * gain1)
        tokv[...] = nn(rt_v[...], gwork.astype(BF16)).astype(BF16).reshape(n, z.cap, d)
        lines[1].start(lambda place: tokv.at[place], back_tok)
        grad_l[:, put_at(late, "db", d)] = tn(rank_b, act1[...]).astype(BF16)
        grad_l[:, put_at(late, "dg", d)] = tn(rank_g, act1[...]).astype(BF16)

    pl.run_scoped(
        branch_pass, V((2, d, w), BF16), V((2, d, w), BF16), V((2, w, 2 * DH), BF16), V((2, LIVE, w), F32),
        V((LIVE, w), BF16), V((LIVE, d), BF16), V((LIVE, d), BF16), V((2, LIVE, NAR), F32), DMA((2, 4)), DMA((2,)),
    )
    red_l.to_core()
    keep_tok = pltpu.make_async_copy(tokv.at[s], back_tok.at[s], lsem.at[0, 2])
    keep_tok.start()
    red_e.to_second()
    red_f.to_plane()
    red_l.to_first()
    red_e.to_line()
    red_f.over()
    red_l.to_second()
    red_e.to_plane()
    red_f.last()
    red_l.to_line()
    red_e.over()
    red_l.to_plane()
    red_e.last()
    red_l.over()
    red_l.last()
    for red in (red_f, red_e, red_l):
        red.end()
    for line in lines:
        line.arrived()
        line.sent()
    keep.wait()
    keep_tok.wait()


def run_second(z, clusters, *args):
    n, w, d = z.n, z.w, z.d
    S, V = jax.ShapeDtypeStruct, pltpu.VMEM
    cols = [z.ffn_cols, early_table(z)[1], late_table(z)[1]]
    rows, half = NAR // n, NAR // 2
    outs = [S((n, z.cap, d), BF16)] * 2 + [S((rows, c), BF16) for c in cols]
    scratch = [
        V((LIVE, NAR), jnp.int32), V((LIVE, NAR), F32), V((n, 16, w), BF16), V((NAR, z.rec_cols), BF16), V((LIVE, d), BF16),
        V((n, LIVE, w), F32), V((n, LIVE, 2 * w), BF16), V((n, LIVE, w), BF16), V((LIVE, w), F32), V((LIVE, NAR), F32),
        V((2, LIVE, NAR), BF16), V((LIVE, d), F32), V((n, z.cap, d), BF16), V((NAR, cols[1]), BF16), V((NAR, cols[2]), BF16),
        V((4, NAR, cols[0] // PLANE), BF16),
    ]
    more = clusters > 1
    for size in cols:
        c = size // PLANE
        scratch += [
            V((4, NAR, c), BF16), V((2, 2, half, c), BF16), V((2 if more else 1, NAR, c), BF16),
            V((clusters, NAR, c) if more else (1, 16, 128), BF16), V((n, rows, c), BF16), V((rows, c), BF16),
        ]
    scratch += [DMA((3, 10)), DMA((3, 10)), DMA((3, n)), DMA((3, n)), DMA((3, clusters)), DMA((3, clusters)), DMA((3, 7)), DMA((3, 7))]
    scratch += [DMA((2, n)), DMA((2, n)), DMA((3, max(n, 4)))]
    SM = pl.BlockSpec(memory_space=pltpu.SMEM)
    return pl.pallas_call(
        functools.partial(second_kernel, z, clusters),
        out_shape=outs,
        in_specs=[SM, SM, VM, VM, VM] + [ANY] * (len(args) - 5),
        out_specs=[ANY, ANY, VM, VM, VM],
        scratch_shapes=scratch,
        compiler_params=pltpu.CompilerParams(collective_id=2, has_side_effects=True, vmem_limit_bytes=VLIMIT),
        name="second",
    )(*args)


def local(
    tokens, cotangent, norm_first, branch_weight, gelu_weight, conv_weight, conv_bias, gate_weight, gate_bias,
    decay_param, merge_weight, norm_second, feed_gate, feed_up, feed_down, down_branch, up_branch, down_gelu,
    up_gelu, down_gates, up_gates, down_merge, up_merge, down_feed_gate, up_feed_gate, down_feed_up, up_feed_up,
    down_feed_down, up_feed_down, seq_lengths, adapter_index, deal_order,
):
    n = lax.axis_size("shard")
    clusters = lax.axis_size("rep") // PLANE
    rows, d = tokens.shape
    z = Sizes(n, d, branch_weight.shape[1] * n, feed_gate.shape[1] * n, rows)
    w, pad = z.w, z.hp - z.h

    def spaced(values):
        if pad == 0:
            return values
        parts = values.reshape(values.shape[0], n, z.h)
        return jnp.pad(parts, ((0, 0), (0, 0), (0, pad))).reshape(values.shape[0], n * z.hp)

    rec_own = (down_branch.T, down_gelu.T, down_gates.T, down_merge.T, up_branch, up_gelu, up_gates, up_merge)
    ffn_own = (
        down_feed_gate.T, down_feed_up.T, spaced(down_feed_down.T), spaced(up_feed_gate), spaced(up_feed_up), up_feed_down
    )

    def gain(values):
        return jnp.pad(values, (0, w - values.shape[0]))

    small = jnp.concatenate(
        [conv_weight.reshape(-1), conv_bias, decay_param, gate_bias.reshape(-1), gain(norm_first), gain(norm_second), jnp.zeros((6 * w,), BF16)]
    ).reshape(16, w)
    gates = gate_weight.reshape(w, 2 * DH)
    arrays = [branch_weight, gelu_weight, gates, None, merge_weight, feed_gate, feed_up, None, feed_down]
    sizes = [x.shape[0] if x is not None else 0 for x in arrays]
    geo = [(0, size // PLANE) for size in sizes]
    geo[3], geo[7] = (1, z.rec_cols // PLANE), (1, z.ffn_cols // PLANE)
    weights = (branch_weight, gelu_weight, gates, merge_weight)
    got = run_first(
        z, geo, seq_lengths, adapter_index, deal_order, small, tokens, cotangent, *weights, feed_gate, feed_up, feed_down,
        *rec_own, *ffn_own,
    )
    gb, gg, ggw, gr, gm, _, _, _, _, _, _, sm = got[:12]
    act1, xin, mixed, ranks, rt, order = got[12:18]
    saved = got[18:23]
    out_send, gres, grad_ffn = got[23:]
    back_out, back_tok, fin_f, fin_e, fin_l = run_second(
        z, clusters, seq_lengths, adapter_index, rt, gres, ranks, sm, *weights, gb, gg, ggw, gm, gr, *saved, act1, xin, mixed,
        out_send.reshape(n, z.cap, d), grad_ffn,
    )

    def arrival(received):
        return tn(order, received.reshape(rows, d))

    (early, _), (late, _) = early_table(z), late_table(z)

    def part(values, table, name, size):
        return values[:, table[name] : table[name] + size].astype(F32)

    def unspaced(values):
        if pad == 0:
            return values
        return values.reshape(values.shape[0], n, z.hp)[:, :, : z.h].reshape(values.shape[0], n * z.h)

    lru, ffp = n * w, n * z.hp
    return (
        arrival(back_out),
        arrival(back_tok),
        part(fin_l, late, "db", d).T,
        part(fin_l, late, "ub", lru),
        part(fin_l, late, "dg", d).T,
        part(fin_l, late, "ug", lru),
        part(fin_l, late, "dgates", lru).T,
        part(fin_e, early, "ugates", 2 * lru),
        part(fin_e, early, "dm", lru).T,
        part(fin_e, early, "um", d),
        part(fin_f, z.ffn, "dfg", d).T,
        unspaced(part(fin_f, z.ffn, "ufg", ffp)),
        part(fin_f, z.ffn, "dfu", d).T,
        unspaced(part(fin_f, z.ffn, "ufu", ffp)),
        unspaced(part(fin_f, z.ffn, "dfd", ffp)).T,
        part(fin_f, z.ffn, "ufd", d),
    )


def solution(mesh):
    tok, line, col, row = P(("rep", "shard"), None), P("shard"), P(None, "shard"), P("shard", None)
    in_specs = (
        tok, tok, line, col, col, col, line, P("shard", None, None), row, line, row, line, col, col, row,
    ) + (col, row) * 7 + (tok, tok, P("rep", None))
    out_specs = (tok, tok) + (col, row) * 7
    return jax.shard_map(local, mesh=mesh, in_specs=in_specs, out_specs=out_specs, check_vma=False)
```

time: 3020 us -> 458 us (0.15)
  waiting for transfers between devices: 1740 us -> 0 us
  local copies, waits for them, and re-layouts: 544 us -> 5.55 us
  Pallas kernels: 0 us -> 431 us
  blocking collectives: 295 us -> 0 us
  matrix products: 234 us -> 5.34 us
  other arithmetic: 177 us -> 8.81 us
    all_gather x15 -> x0, waiting for transfers between devices: 1210 us -> none  [the longest x1 234 us: local(): lax.all_gather(feed_down, 'shard', axis=0, tiled=True)]
    psum x1 -> x0, waiting for transfers between devices: 528 us -> none  [local(): lax.psum((grad_down_branch, grad_up_branch, grad_down_gelu, grad_up_gelu,...]
    pallas_call x0 -> x2, Pallas kernels: none -> 431 us  [the longest x1 319 us: run_first(): pl.pallas_call(functools.partial(first_kernel, z, geo), out_shape=outs, i...]
    all_gather x16 -> x0, blocking collectives: 295 us -> none  [the longest x1 24.9 us: local(): lax.all_gather(down_merge, 'shard', axis=1, tiled=True)]
    pad x70 -> x2, local copies, waits for them, and re-layouts: 244 us -> 1.37 us  [gain(): return jnp.pad(values, (0, w - values.shape[0]))]
    dot_general x56 -> x2, matrix products: 234 us -> 5.34 us  [tn(): lax.dot_general(a, b, (((0,), (0,)), ((), ())), preferred_element_type=F32)]
    slice x71 -> x0, local copies, waits for them, and re-layouts: 178 us -> none  [the longest x69 178 us: recurrence(): unused, state = lax.associative_scan(combine, (carried, driven), axis=0)]
    mul x21 -> x0, other arithmetic: 62.9 us -> none  [the longest x15 22.1 us: combine(): return (earlier[0] * later[0], later[0] * earlier[1] + later[1])]
  transfers between devices with their start and end apart: 16 -> 0, of which waited for: 11 -> 0; matrix products, arithmetic and copies ran while one was open for 16% -> 0% of each run, Pallas kernels for 0% -> 0%
where the time goes in v2:
time: 458 us; the launch traced here: 452 us
  Pallas kernels  431 us (94%)
  other arithmetic  8.81 us (2%)
  local copies, waits for them, and re-layouts  5.55 us (1%)
  matrix products  5.34 us (1%)
    pallas_call x1, Pallas kernels, run_first(): pl.pallas_call(functools.partial(first_kernel, z, geo), out_shape=outs, i...  319 us
    pallas_call x1, Pallas kernels, run_second(): pl.pallas_call(functools.partial(second_kernel, z, clusters), out_shape=o...  112 us

profile of v2, /device:TPU:0, one launch (start us, length us, event | category | flops | bytes accessed | tf_op | source)
XLA Modules:
  0.0 451.6 jit_solution(18305198203515560322)
XLA Ops:
  0.6 0.7 pad.7
  1.3 0.7 pad.8
  2.0 0.7 copy.49
  2.7 0.7 copy.48
  3.4 0.9 dynamic-update-slice.1
  4.3 0.9 dynamic-update-slice.2
  5.1 0.2 dynamic-update-slice.4
  5.3 0.2 dynamic-update-slice.5
  5.6 0.6 reshape.55.refs_3_
  6.2 318.7 %first.1 = (bf16[4,1536,512]{2,1,0:T(8,128)(2,1)}, bf16[4,1536,512]{2,1,0:T(8,128)(2,1)}, bf16[4,512,256]{2,1,0:T(8,128)(2,1)}, bf16[4,32,17408]{2,1,0:T(8,128)(...) custom-call(s32[1,4]{1,0:T(1,128)} %refs_0_.3, ...), custom_call_target="tpu_custom_call" | custom-call | tf_op jit(solution)/shard_map/first/pallas_call | solution.py:793
  324.9 112.0 %second.1 = (bf16[4,128,1536]{2,1,0:T(8,128)(2,1)}, bf16[4,128,1536]{2,1,0:T(8,128)(2,1)}, bf16[32,18432]{1,0:T(8,128)(2,1)}, bf16[32,8192]{1,0:T(8,128)(2,1)}, bf16[32,9216]{1,0:T(8,128)(2,1)}) custom-call(s32[1,4]{1,0:T(1,128)} %refs_0_.3, s32[1,4]{1,0:T(1,128)} %refs_1_.3, bf16[512,384]{1,0:T(8,128)(2,1)} %get-tuple-element.42.refs_2_, ...), custom_call_target="tpu_custom_call" | custom-call | tf_op jit(solution)/shard_map/second/pallas_call | solution.py:1192
  436.9 0.0 copy-start.3
  436.9 1.7 slice_convert_fusion.6
  438.6 1.8 slice_convert_fusion.2
  440.4 2.1 convert_bitcast_fusion.2
  442.5 0.0 copy-start
  442.5 0.0 copy-start.2
  442.5 0.0 copy-done.3
  442.5 2.0 convert_bitcast_fusion.5
  444.5 1.2 convert_bitcast_fusion
  445.8 0.0 copy-done
  445.8 0.0 copy-done.2
  445.8 0.0 copy-start.1
  445.8 2.7 fusion.1
  448.4 0.0 copy-done.1
  448.4 2.7 fusion
  (3 shorter events, 0.0 us)
Async XLA Ops:
  436.9 5.5 %copy-start.3 = (bf16[32,18432]{1,0:T(8,128)(2,1)S(1)}, bf16[32,18432]{1,0:T(8,128)(2,1)}, u32[]{:S(2)}) copy-start(bf16[32,18432]{1,0:T(8,128)(2,1)} %get-tuple-element.65) | copy-start | bytes 3538948
  442.5 3.3 copy-start
  442.5 3.3 copy-start.2
  445.8 2.7 copy-start.1

commit v3 on v2

--- a/solution.py
+++ b/solution.py
@@ -240,9 +240,13 @@
 
     def line(self, a, t):
         for up in (True, False):
-            came, goes, copy = self.forward(a, t, up)
-            pl.when(came)(lambda: copy.wait_recv())
-            pl.when(goes)(lambda: self.forward(a, t, up)[2].start())
+            _, goes, _ = self.forward(a, t, up)
+
+            @pl.when(goes)
+            def _():
+                copy = self.forward(a, t, up)[2]
+                copy.wait_recv()
+                copy.start()
 
     def send(self, view, a, j, k, kind, bit):
         remote(view, view, self.sp.at[kind, a, k - 1], self.rp.at[kind, a, j], self.at.across(bit)).start()
@@ -256,6 +260,11 @@
     def spread(self, a, k):
         j = self.place(k)
         view = self.got(a, j, self.at.p)
+
+        @pl.when((self.at.s == 0) | (self.at.s == self.at.n - 1))
+        def _():
+            remote(view, view, self.sz.at[0, a], self.rz.at[a, j], self.at.across(1)).wait_recv()
+
         self.send(view, a, j, k, 0, 2)
         self.send(view, a, j, k, 1, 4)
         self.send(view, a, j, k, 3, 1)
@@ -462,10 +471,6 @@
             for r in range(1, n):
                 if (r - 1) % 3 == (4, 7, 10).index(i):
                     lines[0].start(lambda place: rows_out.at[0, place], gtok, r)
-        if i >= count - 3:
-            for r in range(1, n):
-                if (r - 1) % 3 == i - count + 3:
-                    lines[1].start(lambda place: rows_out.at[1, place], gcot, r)
         if i + 3 < len(rec):
             net.own(rec[i + 3])
         if i == len(rec):
@@ -578,7 +583,7 @@
             pltpu.make_async_copy(gi.at[j], gi_h.at[j], hsem.at[1, j]).start()
             acc[...] += nt(cl[j], adp[:, cols("dgates", w, j)])
             for i, a in enumerate(ffn):
-                @pl.when(j == i + 1)
+                @pl.when(j == i)
                 def _():
                     if n > 2:
                         net.line(a, 2)
@@ -586,6 +591,7 @@
             return carry
 
         lax.fori_loop(0, n, first_pass, 0)
+        lines[1].start(lambda place: rows_out.at[1, place], gcot)
         ranks[2] = (acc[...] * mask).astype(BF16)
         acc[...] = jnp.zeros_like(acc)
         holds = (ig_h, rg_h, st_h)
@@ -676,43 +682,55 @@
         weights = ((5, ofg, gfg, wg), (6, ofu, gfu, wu), (8, ofd, gfd, wd))
         for k in range(1, n):
             net.ready(7, k)
-        lines[1].arrived()
-        rows_of(1, gcot, tok, tsem.at[0])
-        gl[...] = tn(rt_v[...], tok[...]).astype(BF16)
-
-        def tick(i, q):
-            a = ffn[i]
-
-            @pl.when(q + 3 < n)
-            def _():
-                net.spread(a, q + 3)
-
-            @pl.when(q + 4 < n)
-            def _():
-                net.line(a, q + 4)
-
-            @pl.when(q + 2 < n)
-            def _():
-                net.corner(a, q + 2)
-
-            @pl.when(q + 1 < n)
-            def _():
-                net.twin(a, q + 1)
+
+        def onward(q):
+            for a in ffn:
+                @pl.when(q + 3 < n)
+                def _():
+                    net.spread(a, q + 3)
+
+                @pl.when(q + 4 < n)
+                def _():
+                    net.line(a, q + 4)
+
+        def settle(q):
+            for a in ffn:
+                @pl.when(q + 1 < n)
+                def _():
+                    net.twin(a, q + 1)
+
+            for a in ffn:
+                @pl.when(q + 2 < n)
+                def _():
+                    net.corner(a, q + 2)
 
         def step(q, carry):
             j = jnp.where(q == 0, s, item(jnp.maximum(q, 1), s, n)[0])
-            for i, (a, mine, got, into) in enumerate(weights):
+            def fetch(i):
+                a, mine, got, into = weights[i]
+
                 @pl.when(q > 0)
                 def _():
                     net.ready(a, q)
                     pltpu.make_async_copy(got.at[j], into, wsem.at[i]).start()
 
+            fetch(0)
+            fetch(1)
+            pl.when(q < n - 1)(lambda: fetch(2))
             fg, fu, fd = cols("ufg", h, j, hp), cols("ufu", h, j, hp), cols("dfd", h, j, hp)
             pltpu.make_async_copy(ofg, wg, wsem.at[0]).wait()
             hgs[...] = nn(act2[...], wg[...]) + nn(rk[0], adp[:, fg])
+            onward(q)
             pltpu.make_async_copy(ofu, wu, wsem.at[1]).wait()
             hus[...] = nn(act2[...], wu[...]) + nn(rk[1], adp[:, fu])
-            tick(0, q)
+            @pl.when(q == 0)
+            def _():
+                lines[1].arrived()
+                rows_of(1, gcot, tok, tsem.at[0])
+                gl[...] = tn(rt_v[...], tok[...]).astype(BF16)
+                rk[2] = (nt(gl[...], adp[:, cols("ufd", d)]) * mask).astype(BF16)
+
+            pl.when(q == n - 1)(lambda: fetch(2))
             pltpu.make_async_copy(ofd, wd, wsem.at[2]).wait()
             ghs[...] = nt(gl[...], wd[...]) + nn(rk[2], adp[:, fd])
 
@@ -726,16 +744,15 @@
                 return carry
 
             lax.fori_loop(0, LIVE // 16, block, 0)
-            tick(1, q)
             acc_o[...] += nn(low[...], wd[...])
             ra[0] += nt(low[...], adp[:, fd])
             ra[1] += nt(ghg[...], adp[:, fg])
             ra[2] += nt(ghu[...], adp[:, fu])
-            tick(2, q)
             acc_g[...] += nt(ghg[...], wg[...]) + nt(ghu[...], wu[...])
             grad_o[:, fd] = tn(rk[2], low[...]).astype(BF16)
             grad_o[:, fg] = tn(rk[0], ghg[...]).astype(BF16)
             grad_o[:, fu] = tn(rk[1], ghu[...]).astype(BF16)
+            settle(q)
             return carry
 
         adp_in = load_pack(pack_f, gf, adp, tsem.at[1])
@@ -745,7 +762,6 @@
             copy.wait()
         rk[0] = (nt(act2[...], adp[:, cols("dfg", d)]) * mask).astype(BF16)
         rk[1] = (nt(act2[...], adp[:, cols("dfu", d)]) * mask).astype(BF16)
-        rk[2] = (nt(gl[...], adp[:, cols("ufd", d)]) * mask).astype(BF16)
         lax.fori_loop(0, n, step, 0)
         rank = (ra[0] * mask).astype(BF16)
         work = resid[...] + acc_o[...] + nn(rank, adp[:, cols("ufd", d)])
@@ -825,6 +841,7 @@
         p = at.p
         self.core, self.x, self.y = p % 2, (p // 2) % 2, p // 4
         self.rows, self.half = NAR // at.n, NAR // 2
+        self.final = 1 if clusters > 1 else 0
 
     def cut(self, q):
         return pl.ds(pl.multiple_of(q * self.c, 128), self.c)
@@ -877,7 +894,6 @@
             add_rows(self.r2.at[1], self.rg.at[0], self.rg.at[1], NAR)
             for other in range(2, self.clusters):
                 add_rows(self.r2.at[1], self.rg.at[other], self.r2.at[1], NAR)
-        self.final = 1 if self.clusters > 1 else 0
         for r in range(1, at.n):
             d = lax.rem(at.s + r, at.n)
             chunk = pl.ds(pl.multiple_of(d * self.rows, self.rows), self.rows)
@@ -1059,6 +1075,8 @@
             lax.fori_loop(0, blocks, block, jnp.zeros((8, w), F32))
             acc[...] += nt(glow[j], adp[:, cols("ugates", 2 * w, j)])
             grad_e[:, put_at(early, "ugates", 2 * w, j)] = tn(ranks[2], glow[j]).astype(BF16)
+            pl.when(j == 1)(red_f.to_second)
+            pl.when(j == 2)(red_f.to_line)
             return carry
 
         lax.fori_loop(0, n, body, 0)
@@ -1079,7 +1097,6 @@
         load(jnp.int32(0), 0)
         for copy in ends:
             copy.start()
-        red_f.to_second()
         accg[...] = jnp.zeros_like(accg)
         grads_rank[...] = jnp.zeros_like(grads_rank)
 
@@ -1121,7 +1138,8 @@
             grads_rank[0] += nt(blow[...], adp[:, cols("ub", w, j)])
             grads_rank[1] += nt(gil, adp[:, cols("ug", w, j)])
             pl.when(j == 0)(red_e.to_first)
-            pl.when(j == n - 1)(red_f.to_line)
+            pl.when(j == 2)(red_e.to_second)
+            pl.when(j == 3)(red_e.to_line)
             return carry
 
         lax.fori_loop(0, n, body, 0)
@@ -1144,18 +1162,16 @@
     red_l.to_core()
     keep_tok = pltpu.make_async_copy(tokv.at[s], back_tok.at[s], lsem.at[0, 2])
     keep_tok.start()
-    red_e.to_second()
+    red_l.to_first()
     red_f.to_plane()
-    red_l.to_first()
-    red_e.to_line()
+    red_l.to_second()
     red_f.over()
-    red_l.to_second()
     red_e.to_plane()
+    red_l.to_line()
     red_f.last()
-    red_l.to_line()
     red_e.over()
+    red_e.last()
     red_l.to_plane()
-    red_e.last()
     red_l.over()
     red_l.last()
     for red in (red_f, red_e, red_l):

time: 458 us -> 434 us (0.948)
  Pallas kernels: 431 us -> 407 us
    pallas_call x1, Pallas kernels: 319 us -> 296 us  [run_first(): pl.pallas_call(functools.partial(first_kernel, z, geo), out_shape=outs, i...]
where the time goes in v3:
time: 434 us; the launch traced here: 428 us
  Pallas kernels  407 us (94%)
  other arithmetic  8.81 us (2%)
  local copies, waits for them, and re-layouts  5.55 us (1%)
  matrix products  5.34 us (1%)
    pallas_call x1, Pallas kernels, run_first(): pl.pallas_call(functools.partial(first_kernel, z, geo), out_shape=outs, i...  296 us
    pallas_call x1, Pallas kernels, run_second(): pl.pallas_call(functools.partial(second_kernel, z, clusters), out_shape=o...  111 us

profile of v3, /device:TPU:0, one launch (start us, length us, event | category | flops | bytes accessed | tf_op | source)
XLA Modules:
  0.0 428.0 jit_solution(9883658285021295564)
XLA Ops:
  0.6 0.7 pad.7
  1.3 0.7 pad.8
  2.0 0.7 copy.49
  2.7 0.7 copy.48
  3.4 0.9 dynamic-update-slice.1
  4.3 0.9 dynamic-update-slice.2
  5.1 0.2 dynamic-update-slice.4
  5.3 0.2 dynamic-update-slice.5
  5.6 0.6 reshape.55.refs_3_
  6.2 296.5 %first.1 = (bf16[4,1536,512]{2,1,0:T(8,128)(2,1)}, bf16[4,1536,512]{2,1,0:T(8,128)(2,1)}, bf16[4,512,256]{2,1,0:T(8,128)(2,1)}, bf16[4,32,17408]{2,1,0:T(8,128)(...) custom-call(s32[1,4]{1,0:T(1,128)} %refs_0_.3, ...), custom_call_target="tpu_custom_call" | custom-call | tf_op jit(solution)/shard_map/first/pallas_call | solution.py:809
  302.7 110.9 %second.1 = (bf16[4,128,1536]{2,1,0:T(8,128)(2,1)}, bf16[4,128,1536]{2,1,0:T(8,128)(2,1)}, bf16[32,18432]{1,0:T(8,128)(2,1)}, bf16[32,8192]{1,0:T(8,128)(2,1)}, bf16[32,9216]{1,0:T(8,128)(2,1)}) custom-call(s32[1,4]{1,0:T(1,128)} %refs_0_.3, s32[1,4]{1,0:T(1,128)} %refs_1_.3, bf16[512,384]{1,0:T(8,128)(2,1)} %get-tuple-element.42.refs_2_, ...), custom_call_target="tpu_custom_call" | custom-call | tf_op jit(solution)/shard_map/second/pallas_call | solution.py:1208
  413.6 0.0 copy-start.3
  413.6 1.7 slice_convert_fusion.6
  415.3 1.8 slice_convert_fusion.2
  417.1 2.1 convert_bitcast_fusion.2
  419.1 0.0 copy-start
  419.1 0.0 copy-start.2
  419.1 0.0 copy-done.3
  419.1 2.0 convert_bitcast_fusion.5
  421.2 1.2 convert_bitcast_fusion
  422.4 0.0 copy-done
  422.4 0.0 copy-done.2
  422.4 0.0 copy-start.1
  422.4 2.7 fusion.1
  425.1 0.0 copy-done.1
  425.1 2.7 fusion
  (3 shorter events, 0.0 us)
Async XLA Ops:
  413.6 5.5 %copy-start.3 = (bf16[32,18432]{1,0:T(8,128)(2,1)S(1)}, bf16[32,18432]{1,0:T(8,128)(2,1)}, u32[]{:S(2)}) copy-start(bf16[32,18432]{1,0:T(8,128)(2,1)} %get-tuple-element.65) | copy-start | bytes 3538948
  419.1 3.3 copy-start
  419.1 3.3 copy-start.2
  422.4 2.7 copy-start.1

commit v4 on v3

--- a/solution.py
+++ b/solution.py
@@ -475,8 +475,8 @@
             net.own(rec[i + 3])
         if i == len(rec):
             net.own(7)
-        if 0 <= i - 9 < len(ffn):
-            net.own(ffn[i - 9])
+        if 0 <= i - 12 < len(ffn):
+            net.own(ffn[i - 12])
         net.line(*items[i])
         net.spread(*items[i])
         if i >= 2 and items[i - 2][0] not in ffn:
@@ -591,7 +591,6 @@
             return carry
 
         lax.fori_loop(0, n, first_pass, 0)
-        lines[1].start(lambda place: rows_out.at[1, place], gcot)
         ranks[2] = (acc[...] * mask).astype(BF16)
         acc[...] = jnp.zeros_like(acc)
         holds = (ig_h, rg_h, st_h)
@@ -646,6 +645,7 @@
             return carry
 
         lax.fori_loop(0, n, second_pass, 0)
+        lines[1].start(lambda place: rows_out.at[1, place], gcot)
         put(mix, mixed_h)
         ranks[3] = (acc[...] * mask).astype(BF16)
         put(ranks, ranks_h)
@@ -1035,7 +1035,6 @@
         acc[...] = jnp.zeros_like(acc)
         for copy in own_in:
             copy.wait()
-        red_f.to_first()
 
         def body(j, carry):
             slot = lax.rem(j, 2)
@@ -1075,8 +1074,9 @@
             lax.fori_loop(0, blocks, block, jnp.zeros((8, w), F32))
             acc[...] += nt(glow[j], adp[:, cols("ugates", 2 * w, j)])
             grad_e[:, put_at(early, "ugates", 2 * w, j)] = tn(ranks[2], glow[j]).astype(BF16)
-            pl.when(j == 1)(red_f.to_second)
-            pl.when(j == 2)(red_f.to_line)
+            pl.when(j == 0)(red_f.to_first)
+            pl.when(j == 2)(red_f.to_second)
+            pl.when(j == 3)(red_f.to_line)
             return carry
 
         lax.fori_loop(0, n, body, 0)

time: 434 us -> 433 us (level)
  no operation moved by 1% of the time
where the time goes in v4:
time: 433 us; the launch traced here: 428 us
  Pallas kernels  407 us (94%)
  other arithmetic  8.81 us (2%)
  local copies, waits for them, and re-layouts  5.55 us (1%)
  matrix products  5.34 us (1%)
    pallas_call x1, Pallas kernels, run_first(): pl.pallas_call(functools.partial(first_kernel, z, geo), out_shape=outs, i...  297 us
    pallas_call x1, Pallas kernels, run_second(): pl.pallas_call(functools.partial(second_kernel, z, clusters), out_shape=o...  110 us

profile of v4, /device:TPU:0, one launch (start us, length us, event | category | flops | bytes accessed | tf_op | source)
XLA Modules:
  0.0 427.6 jit_solution(8750200557445630303)
XLA Ops:
  0.6 0.7 pad.7
  1.3 0.7 pad.8
  2.0 0.7 copy.49
  2.7 0.7 copy.48
  3.4 0.9 dynamic-update-slice.1
  4.3 0.9 dynamic-update-slice.2
  5.1 0.2 dynamic-update-slice.4
  5.3 0.2 dynamic-update-slice.5
  5.6 0.6 reshape.55.refs_3_
  6.2 296.5 %first.1 = (bf16[4,1536,512]{2,1,0:T(8,128)(2,1)}, bf16[4,1536,512]{2,1,0:T(8,128)(2,1)}, bf16[4,512,256]{2,1,0:T(8,128)(2,1)}, bf16[4,32,17408]{2,1,0:T(8,128)(...) custom-call(s32[1,4]{1,0:T(1,128)} %refs_0_.3, ...), custom_call_target="tpu_custom_call" | custom-call | tf_op jit(solution)/shard_map/first/pallas_call | solution.py:809
  302.7 110.4 %second.1 = (bf16[4,128,1536]{2,1,0:T(8,128)(2,1)}, bf16[4,128,1536]{2,1,0:T(8,128)(2,1)}, bf16[32,18432]{1,0:T(8,128)(2,1)}, bf16[32,8192]{1,0:T(8,128)(2,1)}, bf16[32,9216]{1,0:T(8,128)(2,1)}) custom-call(s32[1,4]{1,0:T(1,128)} %refs_0_.3, s32[1,4]{1,0:T(1,128)} %refs_1_.3, bf16[512,384]{1,0:T(8,128)(2,1)} %get-tuple-element.42.refs_2_, ...), custom_call_target="tpu_custom_call" | custom-call | tf_op jit(solution)/shard_map/second/pallas_call | solution.py:1208
  413.2 0.0 copy-start.3
  413.2 1.7 slice_convert_fusion.6
  414.9 1.8 slice_convert_fusion.2
  416.6 2.1 convert_bitcast_fusion.2
  418.7 0.0 copy-start
  418.7 0.0 copy-start.2
  418.7 0.0 copy-done.3
  418.7 2.0 convert_bitcast_fusion.5
  420.8 1.2 convert_bitcast_fusion
  422.0 0.0 copy-done
  422.0 0.0 copy-done.2
  422.0 0.0 copy-start.1
  422.0 2.7 fusion.1
  424.7 0.0 copy-done.1
  424.7 2.7 fusion
  (3 shorter events, 0.0 us)
Async XLA Ops:
  413.2 5.5 %copy-start.3 = (bf16[32,18432]{1,0:T(8,128)(2,1)S(1)}, bf16[32,18432]{1,0:T(8,128)(2,1)}, u32[]{:S(2)}) copy-start(bf16[32,18432]{1,0:T(8,128)(2,1)} %get-tuple-element.65) | copy-start | bytes 3538948
  418.7 3.3 copy-start
  418.7 3.3 copy-start.2
  422.0 2.7 copy-start.1
